TPU v7x, 32 devices: a whole 2x2x4 slice. The times are simulated.
32 devices in a mesh: band: 4 (over y, x), tm: 8 (over z, core).
Axes of the slice: x: 2, y: 2, z: 4, core: 2. Of those that a mesh axis runs over, the one named last changes fastest.
Arguments:
- timeline: bfloat16 [4096, 1024], P('tm', 'band'), parts along dimension 1, may hold values from -6 to 6
- pointing: int32 [4096, 1024], P('tm', 'band'), parts along dimension 1, may hold values from 0 to 127
- plate_angle: float32 [4096], P('tm'), may hold values from -3.140625 to 3.140625
- detector_angle: float32 [1024], P('band'), parts along dimension 0, may hold values from -3.140625 to 3.140625
- detector_weight: float32 [1024], P('band'), parts along dimension 0, may hold values from 0.3 to 3
- kernel: bfloat16 [4100], P('band'), parts along dimension 0, may hold values from -0.1875 to 0.1875
- tile_owner: int32 [512, 4], P('tm', 'band'), parts along dimension 1, may hold values from 0 to 7; in each aligned block of 64 rows (0 to 63, 64 to 127, ...) at most 16 rows name the same one
- tile_block: int32 [512, 4], P('tm', 'band'), parts along dimension 1, may hold values from 0 to 8191
- wiener: float32 [12, 4096, 2048], P('band', 'tm'), parts along dimension 0, may hold values from 0.05 to 1
Outputs:
- filtered_spectrum: float32 [2, 12, 4096, 2048], P(None, 'band', 'tm'), parts along dimension 1
There are 4 independent parts, one for each index of `band`. A program takes and returns all parts, laid end to end along the dimension named above; an argument that names none is the same for every part. Nothing has to cross between parts.
Inputs may be any that keep to these rules, and one draw needn't show every extreme that they name: `tile_owner`: at most 16 of the 64 tiles of one time shard name the same owner, some shard's tiles name one owner exactly 16 times, and every owner is named by some tile.
All inputs are finite; a program needn't handle non-finite values.
Results may differ from a plain program's by a relative error of at most 0.0029.
Values may be sent and summed in bfloat16 or wider, within the bound.
No kernel may reach another device: no remote copies, remote signals or barrier semaphores. Data moves between devices by JAX's collectives and lax.ppermute only.
A program may use at most 192 MiB of HBM per device.

v0:
```python
import math

import jax
import jax.numpy as jnp
from jax import lax
from jax.sharding import PartitionSpec as P

DET = 256
TS = 512
HALF = 512
PIECE = 16
DGRP = 128
BPIX = 128
ROWS = 2048
COLS = 4096
NTILE = 64


def with_halo(value, sides, width):
    for axis, dim in sides:
        size, length = (lax.axis_size(axis), value.shape[dim])
        up = [(i, (i + 1) % size) for i in range(size - 1)]
        down = [(j, i) for i, j in up]
        last = lax.slice_in_dim(value, length - width, length, axis=dim)
        first = lax.slice_in_dim(value, 0, width, axis=dim)
        before = lax.ppermute(last, axis, up)
        after = lax.ppermute(first, axis, down)
        value = jnp.concatenate([before, value, after], axis=dim)
    return value


def band_matrix(kernel):
    half_width = (kernel.shape[0] - 1) // 2
    pattern = jnp.concatenate([kernel, jnp.zeros((half_width,), kernel.dtype)])
    repeated = jnp.tile(pattern, half_width)[: 3 * half_width * half_width]
    return repeated.reshape(half_width, 3 * half_width)


def apply_band(padded, band_rows):
    half_width = band_rows.shape[0]
    blocks = padded.reshape(-1, half_width, padded.shape[1])
    windows = jnp.concatenate([blocks[:-2], blocks[1:-1], blocks[2:]], axis=1)
    result = jnp.einsum("ij,bjc->bic", band_rows, windows, preferred_element_type=jnp.float32)
    return result.reshape(-1, padded.shape[1])


def phase_table(count_rows, count_cols, modulus):
    product = (
        jnp.arange(count_rows, dtype=jnp.int32)[:, None]
        * jnp.arange(count_cols, dtype=jnp.int32)[None, :]
        % modulus
    )
    phases = product.astype(jnp.float32) * (-2.0 * math.pi / modulus)
    return (jnp.cos(phases), jnp.sin(phases))


def contract(spec_text, left_side, right_side):
    return jnp.einsum(spec_text, left_side, right_side, precision=lax.Precision.HIGHEST)


def fourier_last(real_in, imag_in):
    length = real_in.shape[-1]
    outer_len = 1 << (length.bit_length() - 1) // 2
    inner_len = length // outer_len
    leading = real_in.shape[:-1]
    cos_outer, sin_outer = phase_table(outer_len, outer_len, outer_len)
    real_grid = real_in.reshape(leading + (outer_len, inner_len))
    real_mid = contract("...nb,nk->...kb", real_grid, cos_outer)
    imag_mid = contract("...nb,nk->...kb", real_grid, sin_outer)
    if imag_in is not None:
        imag_grid = imag_in.reshape(leading + (outer_len, inner_len))
        real_mid = real_mid - contract("...nb,nk->...kb", imag_grid, sin_outer)
        imag_mid = imag_mid + contract("...nb,nk->...kb", imag_grid, cos_outer)
    cos_twist, sin_twist = phase_table(outer_len, inner_len, length)
    real_turn = real_mid * cos_twist - imag_mid * sin_twist
    imag_turn = real_mid * sin_twist + imag_mid * cos_twist
    cos_inner, sin_inner = phase_table(inner_len, inner_len, inner_len)
    real_out = contract("...kn,nm->...mk", real_turn, cos_inner) - contract(
        "...kn,nm->...mk", imag_turn, sin_inner
    )
    imag_out = contract("...kn,nm->...mk", real_turn, sin_inner) + contract(
        "...kn,nm->...mk", imag_turn, cos_inner
    )
    factor = 1.0 / math.sqrt(length)
    return (
        real_out.reshape(leading + (length,)) * factor,
        imag_out.reshape(leading + (length,)) * factor,
    )


def body(
    timeline,
    pointing,
    plate_angle,
    detector_angle,
    detector_weight,
    kernel,
    tile_owner,
    tile_block,
    wiener,
):
    band_rows = band_matrix(kernel)
    padded = with_halo(timeline, (("tm", 0),), HALF)
    filtered = apply_band(padded, band_rows)
    weighted = detector_weight[None, :] * filtered
    angle = 2.0 * plate_angle[:, None] + detector_angle[None, :]
    stokes = jnp.stack(
        [weighted, weighted * jnp.cos(2.0 * angle), weighted * jnp.sin(2.0 * angle)]
    ).astype(jnp.bfloat16)
    pieces = TS // PIECE
    groups = DET // DGRP
    tile_values = (
        stokes.reshape(3, pieces, PIECE, groups, DGRP)
        .transpose(1, 3, 0, 2, 4)
        .reshape(NTILE, 3, PIECE * DGRP)
    )
    tile_pixels = (
        pointing.reshape(pieces, PIECE, groups, DGRP)
        .transpose(0, 2, 1, 3)
        .reshape(NTILE, PIECE * DGRP)
    )
    low_count = 16
    high_count = BPIX // low_count
    high_ids = jnp.arange(high_count, dtype=jnp.int32)
    low_ids = jnp.arange(low_count, dtype=jnp.int32)
    block_size = NTILE // 8
    block_sums = []
    for first_tile in range(0, NTILE, block_size):
        pixels = tile_pixels[first_tile : first_tile + block_size]
        values = tile_values[first_tile : first_tile + block_size]
        high_hot = ((pixels // low_count)[:, None, :] == high_ids[None, :, None]).astype(
            jnp.bfloat16
        )
        low_hot = ((pixels % low_count)[:, None, :] == low_ids[None, :, None]).astype(jnp.bfloat16)
        spread = values[:, :, None, :] * high_hot[:, None, :, :]
        binned = jnp.einsum("bshn,bln->bshl", spread, low_hot, preferred_element_type=jnp.float32)
        block_sums.append(binned.reshape(block_size, 3 * BPIX))
    tile_sums = jnp.concatenate(block_sums)
    devices = lax.axis_size("tm")
    capacity = max(2, (2 * NTILE + devices - 1) // devices)
    owner_ids = tile_owner[:, 0]
    owner_hot = (owner_ids[:, None] == jnp.arange(devices, dtype=jnp.int32)[None, :]).astype(
        jnp.int32
    )
    earlier = jnp.cumsum(owner_hot, axis=0) - owner_hot
    rank_in = jnp.sum(earlier * owner_hot, axis=1)
    slot_ids = owner_ids * capacity + rank_in
    select = (jnp.arange(devices * capacity, dtype=jnp.int32)[:, None] == slot_ids[None, :]).astype(
        jnp.float32
    )
    outgoing = jnp.dot(select, tile_sums, precision=lax.Precision.HIGHEST)
    labels = jnp.dot(select, (tile_block + 1).astype(jnp.float32), precision=lax.Precision.HIGHEST)[
        :, 0
    ]
    incoming, in_labels = (
        lax.all_to_all(outgoing, "tm", split_axis=0, concat_axis=0, tiled=True),
        lax.all_to_all(labels, "tm", split_axis=0, concat_axis=0, tiled=True),
    )
    rows_own = ROWS // devices
    col_blocks = COLS // BPIX
    owned = rows_own * col_blocks
    collect = (
        jnp.arange(1, owned + 1, dtype=jnp.int32).astype(jnp.float32)[:, None] == in_labels[None, :]
    ).astype(jnp.float32)
    local_map = jnp.dot(collect, incoming, precision=lax.Precision.HIGHEST)
    local_map = (
        local_map.reshape(rows_own, col_blocks, 3, BPIX)
        .transpose(2, 0, 1, 3)
        .reshape(3, rows_own, COLS)
    )
    row_real, row_imag = fourier_last(local_map, None)
    spectra = lax.all_to_all(
        jnp.stack([row_real, row_imag]), "tm", split_axis=3, concat_axis=2, tiled=True
    )
    columns = spectra.transpose(0, 1, 3, 2)
    col_real, col_imag = fourier_last(columns[0], columns[1])
    return jnp.stack([col_real * wiener, col_imag * wiener])


def solution(mesh):
    placed = (
        P("tm", "band"),
        P("tm", "band"),
        P("tm"),
        P("band"),
        P("band"),
        P("band"),
        P("tm", "band"),
        P("tm", "band"),
        P("band", "tm", None),
    )
    return jax.shard_map(
        body, mesh=mesh, in_specs=placed, out_specs=P(None, "band", "tm", None), check_vma=False
    )
```

profile of v0, /device:TPU:0, one launch (start us, length us, event | category | flops | bytes accessed | tf_op | source)
XLA Modules:
  0.0 1229.9 jit_solution(1971688387539246591)
XLA Ops:
  0.0 3.2 collective-permute-start
  3.2 1.3 collective-permute-start.1
  4.5 0.7 fusion.157
  5.3 0.8 select_reduce_fusion
  6.9 1.7 convolution_bitcast_fusion.2
  8.5 7.5 all-to-all-start
  16.1 1.3 reshape.780
  17.5 0.7 add_select_fusion.13
  18.1 0.7 fusion.87
  18.9 0.7 add_select_fusion.15
  19.6 0.7 fusion.86
  20.3 0.7 add_select_fusion.11
  21.0 0.7 fusion.88
  21.8 0.7 add_select_fusion.9
  22.4 0.7 fusion.89
  23.2 0.7 add_select_fusion.7
  23.9 0.7 fusion.90
  25.3 0.7 fusion.91
  26.0 0.7 add_select_fusion.3
  26.7 0.8 fusion.92
  27.5 0.7 add_select_fusion.1
  28.2 0.7 concatenate.13
  29.0 2.5 tile.10
  31.7 1.8 reshape.779
  33.6 4.4 multiply_convert_fusion.1
  38.7 1.3 maximum_bitcast_fusion.2
  40.7 1.4 fusion.46
  42.3 1.4 fusion.43
  43.8 1.4 fusion.49
  46.0 1.3 fusion.55
  49.2 0.9 fusion.118
  50.2 5.1 all-to-all-start.1
  56.7 6.9 all-to-all-done.1
  63.7 8.2 convolution_bitcast_fusion
  71.9 10.7 copy.177
  82.6 25.5 %fusion.24 = f32[64,3,256,64]{2,0,3,1:T(8,128)} fusion(f32[3,256,64,64]{1,3,2,0:T(8,128)} %bitcast.431), kind=kOutput, calls=%fused_computation.36 | convolution fusion | flops 2415976448 | bytes 25165824 | tf_op jit(solution)/shard_map/...nb,nk->...kb/dot_general | solution.py:58
  108.0 32.1 %subtract_bitcast_fusion.1 = (f32[3,256,64,64]{1,2,3,0:T(8,128)}, f32[3,256,64,64]{1,2,3,0:T(8,128)}) fusion(f32[64,3,256,64]{2,0,3,1:T(8,128)} %fusion.24, f32[64,64]{0,1:T(8,128)S(1)} %get-tuple-element.49, f32[64,64]{0,1:T(8,128)S(1)} %get-tuple-element.50, f32[3,256,64,64]{1,3,2,0:T(8,128)} %bitcast.432), kind=kOutput, calls=%fused_computation.11 | convolution fusion | flops 2434850816 | bytes 50364416 | tf_op jit(solution)/shard_map/...nb,nk->...kb/dot_general | solution.py:58
  140.2 25.6 %fusion.18 = f32[64,3,256,64]{2,0,3,1:T(8,128)} fusion(f32[3,256,64,64]{1,2,3,0:T(8,128)} %get-tuple-element.8), kind=kOutput, calls=%fused_computation.30 | convolution fusion | flops 2415976448 | bytes 25165824 | tf_op jit(solution)/shard_map/...kn,nm->...mk/dot_general | solution.py:58
  165.7 18.9 %fusion.16 = f32[64,3,256,64]{2,0,3,1:T(8,128)} fusion(f32[3,256,64,64]{1,2,3,0:T(8,128)S(1)} %copy-done), kind=kOutput, calls=%fused_computation.28 | convolution fusion | flops 2415976448 | bytes 25165824 | tf_op jit(solution)/shard_map/...kn,nm->...mk/dot_general | solution.py:58
  184.7 27.1 %multiply_bitcast_fusion.3 = f32[3,256,64,64]{1,2,3,0:T(8,128)} fusion(f32[64,3,256,64]{2,0,3,1:T(8,128)} %fusion.18, f32[3,256,64,64]{1,2,3,0:T(8,128)S(1)} %bitcast.426), kind=kOutput, calls=%fused_computation.9 | convolution fusion | flops 2422267904 | bytes 37748736 | tf_op jit(solution)/shard_map/...kn,nm->...mk/dot_general | solution.py:58
  211.8 16.4 %copy.182 = f32[3,256,64,64]{1,3,2,0:T(8,128)} copy(f32[3,256,64,64]{1,2,3,0:T(8,128)} %multiply_bitcast_fusion.3) | data formatting | bytes 25165824 | tf_op jit(solution)/shard_map/mul | solution.py:86
  228.2 28.0 %multiply_bitcast_fusion.2 = f32[3,256,64,64]{1,2,3,0:T(8,128)} fusion(f32[64,3,256,64]{2,0,3,1:T(8,128)} %fusion.16, f32[3,256,64,64]{1,2,3,0:T(8,128)} %get-tuple-element.7), kind=kOutput, calls=%fused_computation.8 | convolution fusion | flops 2422267904 | bytes 37748736 | tf_op jit(solution)/shard_map/...kn,nm->...mk/dot_general | solution.py:58
  256.2 16.4 %copy.185 = f32[3,256,64,64]{1,3,2,0:T(8,128)} copy(f32[3,256,64,64]{1,2,3,0:T(8,128)} %multiply_bitcast_fusion.2) | data formatting | bytes 25165824 | tf_op jit(solution)/shard_map/mul | solution.py:87
  272.6 17.1 %pad_maximum_fusion = f32[2,3,256,4096]{2,3,1,0:T(8,128)} fusion(f32[1,3,256,4096]{2,3,1,0:T(8,128)} %bitcast.438, f32[1,3,256,4096]{2,3,1,0:T(8,128)} %bitcast.437), kind=kLoop, calls=%fused_computation | loop fusion | flops 6291456 | bytes 50331648 | tf_op jit(solution)/shard_map/stack | solution.py:173
  289.7 42.0 %copy.186 = f32[2,3,256,4096]{2,0,1,3:T(2,128)} copy(f32[2,3,256,4096]{2,3,1,0:T(8,128)} %pad_maximum_fusion) | data formatting | bytes 50331648 | tf_op jit(solution)/shard_map/stack | solution.py:173
  331.7 6.8 all-to-all-start.2
  338.5 12.6 %copy.196 = f32[3,512,2048]{1,2,0:T(8,128)} copy(f32[3,512,2048]{2,1,0:T(8,128)} %param.17) | data formatting | bytes 25165824 | tf_op args[8]
  351.3 530.7 %all-to-all-done.2 = f32[2,3,256,4096]{2,0,1,3:T(2,128)} async-done(((f32[2,3,256,4096]{2,0,1,3:T(2,128)}), f32[2,3,256,4096]{2,0,1,3:T(2,128)}, u32[]{:S(2)}, u32[]{:S(2)}) %all-to-all-start.2) | async-done | bytes 25165856 | tf_op jit(solution)/shard_map/all_to_all | solution.py:172
  881.9 19.0 %copy.187 = f32[2,3,256,4096]{2,3,1,0:T(8,128)} copy(f32[2,3,256,4096]{2,0,1,3:T(2,128)} %all-to-all-done.2) | data formatting | bytes 50331648 | tf_op jit(solution)/shard_map/all_to_all | solution.py:172
  901.0 24.8 %copy.188 = f32[2,3,8,256,512]{4,3,2,1,0:T(8,128)} copy(f32[2,3,8,256,512]{3,4,2,1,0:T(8,128)} %bitcast.436) | data formatting | bytes 50331648 | tf_op jit(solution)/shard_map/all_to_all | solution.py:172
  925.7 14.3 %fusion.259 = (f32[1,3,512,2048]{2,3,1,0:T(8,128)S(1)}, f32[1,3,512,2048]{2,3,1,0:T(8,128)}) fusion(f32[2,3,512,2048]{2,3,1,0:T(8,128)} %bitcast.435), kind=kLoop, calls=%fused_computation.350 | loop fusion | bytes 50331648 | tf_op jit(solution)/shard_map/slice | solution.py:176
  940.0 18.5 %fusion.10 = f32[32,3,512,64]{2,0,3,1:T(8,128)} fusion(f32[3,512,32,64]{1,3,2,0:T(8,128)S(1)} %bitcast.429), kind=kOutput, calls=%fused_computation.22 | convolution fusion | flops 1207973888 | bytes 25165824 | tf_op jit(solution)/shard_map/...nb,nk->...kb/dot_general | solution.py:58
  958.6 18.6 %fusion.8 = f32[32,3,512,64]{2,0,3,1:T(8,128)} fusion(f32[3,512,32,64]{1,3,2,0:T(8,128)S(1)} %bitcast.430), kind=kOutput, calls=%fused_computation.20 | convolution fusion | flops 1207973888 | bytes 25165824 | tf_op jit(solution)/shard_map/...nb,nk->...kb/dot_general | solution.py:58
  977.2 25.0 %fusion.12 = f32[32,3,512,64]{2,0,3,1:T(8,128)} fusion(f32[3,512,32,64]{1,3,2,0:T(8,128)} %bitcast.433), kind=kOutput, calls=%fused_computation.24 | convolution fusion | flops 1207973888 | bytes 25165824 | tf_op jit(solution)/shard_map/...nb,nk->...kb/dot_general | solution.py:58
  1002.2 42.4 %subtract_bitcast_fusion = (f32[3,512,32,64]{1,2,3,0:T(8,128)}, f32[3,512,32,64]{1,2,3,0:T(8,128)}) fusion(f32[32,64]{0,1:T(8,128)S(1)} %get-tuple-element.51, f32[32,64]{0,1:T(8,128)S(1)} %get-tuple-element.52, f32[32,3,512,64]{2,0,3,1:T(8,128)} %fusion.12, f32[32,3,512,64]{2,0,3,1:T(8,128)} %fusion.8, f32[32,3,512,64]{2,0,3,1:T(8,128)} %fusion.10, ...), kind=kOutput, calls=%fused_computation.7 | convolution fusion | flops 1233139712 | bytes 75513856 | tf_op jit(solution)/shard_map/...nb,nk->...kb/dot_general | solution.py:58
  1044.6 26.0 %fusion = f32[64,3,512,32]{2,0,3,1:T(8,128)} fusion(f32[3,512,32,64]{1,2,3,0:T(8,128)} %get-tuple-element.6), kind=kOutput, calls=%fused_computation.12 | convolution fusion | flops 2415976448 | bytes 25165824 | tf_op jit(solution)/shard_map/...kn,nm->...mk/dot_general | solution.py:58
  1070.6 18.9 %fusion.2 = f32[64,3,512,32]{2,0,3,1:T(8,128)} fusion(f32[3,512,32,64]{1,2,3,0:T(8,128)S(1)} %copy-done.1), kind=kOutput, calls=%fused_computation.14 | convolution fusion | flops 2415976448 | bytes 25165824 | tf_op jit(solution)/shard_map/...kn,nm->...mk/dot_general | solution.py:58
  1089.6 21.3 %multiply_bitcast_fusion = f32[3,512,64,32]{1,2,3,0:T(8,128)} fusion(f32[64,3,512,32]{2,0,3,1:T(8,128)} %fusion, f32[3,512,32,64]{1,2,3,0:T(8,128)S(1)} %bitcast.428), kind=kOutput, calls=%fused_computation.4 | convolution fusion | flops 2422267904 | bytes 37748736 | tf_op jit(solution)/shard_map/...kn,nm->...mk/dot_general | solution.py:58
  1110.9 16.4 %copy.199 = f32[3,512,64,32]{1,3,2,0:T(8,128)} copy(f32[3,512,64,32]{1,2,3,0:T(8,128)} %multiply_bitcast_fusion) | data formatting | bytes 25165824 | tf_op jit(solution)/shard_map/mul | solution.py:87
  1127.2 28.3 %multiply_bitcast_fusion.1 = f32[3,512,64,32]{1,2,3,0:T(8,128)} fusion(f32[64,3,512,32]{2,0,3,1:T(8,128)} %fusion.2, f32[3,512,32,64]{1,2,3,0:T(8,128)} %get-tuple-element.5), kind=kOutput, calls=%fused_computation.5 | convolution fusion | flops 2422267904 | bytes 37748736 | tf_op jit(solution)/shard_map/...kn,nm->...mk/dot_general | solution.py:58
  1155.5 16.4 %copy.195 = f32[3,512,64,32]{1,3,2,0:T(8,128)} copy(f32[3,512,64,32]{1,2,3,0:T(8,128)} %multiply_bitcast_fusion.1) | data formatting | bytes 25165824 | tf_op jit(solution)/shard_map/mul | solution.py:86
  1171.9 18.6 %bitcast_multiply_fusion.1 = (f32[3,512,2048]{1,2,0:T(8,128)S(1)}, f32[3,512,2048]{1,2,0:T(8,128)}) fusion(f32[3,512,2048]{1,2,0:T(8,128)} %copy.196, f32[3,512,64,32]{1,3,2,0:T(8,128)} %copy.195, f32[3,512,64,32]{1,3,2,0:T(8,128)} %copy.199), kind=kLoop, calls=%fused_computation.3 | loop fusion | flops 6291456 | bytes 62914560 | tf_op jit(solution)/shard_map/mul | solution.py:177
  1190.5 14.2 %pad_maximum_fusion.1 = f32[2,3,512,2048]{2,3,1,0:T(8,128)} fusion(f32[1,3,512,2048]{2,3,1,0:T(8,128)} %bitcast.440, f32[1,3,512,2048]{2,3,1,0:T(8,128)S(1)} %bitcast.439), kind=kLoop, calls=%fused_computation.1 | loop fusion | flops 6291456 | bytes 50331648 | tf_op jit(solution)/shard_map/stack | solution.py:177
  1204.7 25.0 %copy.201 = f32[2,3,512,2048]{3,2,1,0:T(8,128)} copy(f32[2,3,512,2048]{2,3,1,0:T(8,128)} %pad_maximum_fusion.1) | data formatting | bytes 50331648 | tf_op jit(solution)/shard_map/stack | solution.py:177
  (99 shorter events, 7.7 us)
Async XLA Ops:
  0.0 33.5 %copy-start.10 = (f32[512]{0:T(512)S(1)}, f32[512]{0:T(512)}, u32[]{:S(2)}) copy-start(f32[512]{0:T(512)} %param.11) | copy-start | bytes 6148
  0.0 33.5 %collective-permute-start = (bf16[512,256]{1,0:T(8,128)(2,1)}, bf16[512,256]{1,0:T(8,128)(2,1)}, u32[]{:S(2)}, u32[]{:S(2)}) collective-permute-start(bf16[512,256]{1,0:T(8,128)(2,1)} %param.9), channel_id=1, source_target_pairs={{0,1},{1,2},{2,3},{3,4},{4,5},{5,6},{6,7},{8,9},{9,10},{10,11},{11... | collective-permute-start | bytes 786440 | tf_op jit(solution)/shard_map/ppermute | solution.py:26
  3.2 30.3 %collective-permute-start.1 = (bf16[512,256]{1,0:T(8,128)(2,1)}, bf16[512,256]{1,0:T(8,128)(2,1)}, u32[]{:S(2)}, u32[]{:S(2)}) collective-permute-start(bf16[512,256]{1,0:T(8,128)(2,1)} %param.9), channel_id=1, source_target_pairs={{1,0},{2,1},{3,2},{4,3},{5,4},{6,5},{7,6},{9,8},{10,9},{11,10},{12... | collective-permute-start | bytes 786440 | tf_op jit(solution)/shard_map/ppermute | solution.py:27
  8.5 41.7 %all-to-all-start = ((f32[8,16,1]{1,2,0:T(1,128)}), f32[8,16,1]{1,2,0:T(1,128)S(1)}, u32[]{:S(2)}, u32[]{:S(2)}) async-start(f32[8,16,1]{1,2,0:T(1,128)} %convolution_bitcast_fusion.2), calls=%async_computation | async-start | bytes 8192 | tf_op jit(solution)/shard_map/all_to_all | solution.py:157
  33.5 13.9 %copy-start.3 = (bf16[8,8,2048]{2,1,0:T(8,128)(2,1)S(1)}, bf16[8,8,2048]{2,1,0:T(8,128)(2,1)}, u32[]{:S(2)}) copy-start(bf16[8,8,2048]{2,1,0:T(8,128)(2,1)} %fusion.91) | copy-start | bytes 786436
  33.5 13.9 %copy-start.8 = (s32[8,2048]{1,0:T(8,128)S(1)}, s32[8,2048]{1,0:T(8,128)}, u32[]{:S(2)}) copy-start(s32[8,2048]{1,0:T(8,128)} %get-tuple-element.37) | copy-start | bytes 196612
  33.5 14.5 %copy-start.2 = (bf16[8,8,2048]{2,1,0:T(8,128)(2,1)S(1)}, bf16[8,8,2048]{2,1,0:T(8,128)(2,1)}, u32[]{:S(2)}) copy-start(bf16[8,8,2048]{2,1,0:T(8,128)(2,1)} %fusion.92) | copy-start | bytes 786436
  33.6 14.5 %copy-start.7 = (s32[8,2048]{1,0:T(8,128)S(1)}, s32[8,2048]{1,0:T(8,128)}, u32[]{:S(2)}) copy-start(s32[8,2048]{1,0:T(8,128)} %get-tuple-element.35) | copy-start | bytes 196612
  38.0 7.4 copy-start.5
  38.0 7.4 copy-start.9
  38.0 8.0 copy-start.4
  38.0 10.6 copy-start.6
  50.2 13.4 %all-to-all-start.1 = ((f32[8,16,384]{2,1,0:T(8,128)}), f32[8,16,384]{2,1,0:T(8,128)S(1)}, u32[]{:S(2)}, u32[]{:S(2)}) async-start(f32[8,16,384]{2,1,0:T(8,128)} %bitcast.38), calls=%async_computation.1 | async-start | bytes 393216 | tf_op jit(solution)/shard_map/all_to_all | solution.py:156
  140.1 25.6 %copy-start = (f32[3,256,64,64]{1,2,3,0:T(8,128)S(1)}, f32[3,256,64,64]{1,2,3,0:T(8,128)}, u32[]{:S(2)}) copy-start(f32[3,256,64,64]{1,2,3,0:T(8,128)} %get-tuple-element.8) | copy-start | bytes 37748740
  140.1 44.5 %slice-start = ((s8[12582912]{0:T(1024)(128)(4,1)}), s8[4194304]{0:T(1024)(128)(4,1)S(1)}, s32[]{:S(2)}) async-start(s8[12582912]{0:T(1024)(128)(4,1)} %bitcast.425), calls=%async_computation.3 | async-start | bytes 8388608
  140.1 44.5 %slice-start.1 = ((s8[12582912]{0:T(1024)(128)(4,1)}), s8[4194304]{0:T(1024)(128)(4,1)S(1)}, s32[]{:S(2)}) async-start(s8[12582912]{0:T(1024)(128)(4,1)} %bitcast.425), calls=%async_computation.4 | async-start | bytes 8388608
  165.7 18.9 %slice-start.2 = ((s8[12582912]{0:T(1024)(128)(4,1)}), s8[4194304]{0:T(1024)(128)(4,1)S(1)}, s32[]{:S(2)}) async-start(s8[12582912]{0:T(1024)(128)(4,1)} %bitcast.425), calls=%async_computation.5 | async-start | bytes 8388608
  331.7 550.2 %all-to-all-start.2 = ((f32[2,3,256,4096]{2,0,1,3:T(2,128)}), f32[2,3,256,4096]{2,0,1,3:T(2,128)}, u32[]{:S(2)}, u32[]{:S(2)}) async-start(f32[2,3,256,4096]{2,0,1,3:T(2,128)} %copy.186), calls=%async_computation.2 | async-start | bytes 50331648 | tf_op jit(solution)/shard_map/all_to_all | solution.py:172
  1044.6 26.0 %copy-start.1 = (f32[3,512,32,64]{1,2,3,0:T(8,128)S(1)}, f32[3,512,32,64]{1,2,3,0:T(8,128)}, u32[]{:S(2)}) copy-start(f32[3,512,32,64]{1,2,3,0:T(8,128)} %get-tuple-element.6) | copy-start | bytes 37748740
  1044.6 44.9 %slice-start.3 = ((s8[12582912]{0:T(1024)(128)(4,1)}), s8[4194304]{0:T(1024)(128)(4,1)S(1)}, s32[]{:S(2)}) async-start(s8[12582912]{0:T(1024)(128)(4,1)} %bitcast.427), calls=%async_computation.6 | async-start | bytes 8388608
  1044.6 44.9 %slice-start.4 = ((s8[12582912]{0:T(1024)(128)(4,1)}), s8[4194304]{0:T(1024)(128)(4,1)S(1)}, s32[]{:S(2)}) async-start(s8[12582912]{0:T(1024)(128)(4,1)} %bitcast.427), calls=%async_computation.7 | async-start | bytes 8388608
  1070.6 18.9 %slice-start.5 = ((s8[12582912]{0:T(1024)(128)(4,1)}), s8[4194304]{0:T(1024)(128)(4,1)S(1)}, s32[]{:S(2)}) async-start(s8[12582912]{0:T(1024)(128)(4,1)} %bitcast.427), calls=%async_computation.8 | async-start | bytes 8388608
where the time goes:
time: 1240 us; the launch traced here: 1230 us
  waiting for transfers between devices  538 us (43%)
  matrix products  379 us (31%)
  local copies, waits for them, and re-layouts  224 us (18%)
  other arithmetic  65.2 us (5%)
  starting transfers between devices  24 us (2%)
    all_to_all x1, waiting for transfers between devices, body(): lax.all_to_all(jnp.stack([row_real, row_imag]), 'tm', split_axis=3, conca...  531 us
    dot_general x14, matrix products, contract(): jnp.einsum(spec_text, left_side, right_side, precision=lax.Precision.HIGH...  356 us
    all_to_all x2, local copies, waits for them, and re-layouts, body(): lax.all_to_all(jnp.stack([row_real, row_imag]), 'tm', split_axis=3, conca...  43.8 us
    another operation x1, local copies, waits for them, and re-layouts, body(): jnp.stack([row_real, row_imag])  42 us
    mul x2, local copies, waits for them, and re-layouts, fourier_last(): imag_out.reshape(leading + (length,)) * factor  32.8 us
    mul x2, local copies, waits for them, and re-layouts, fourier_last(): real_out.reshape(leading + (length,)) * factor  32.8 us
    another operation x1, local copies, waits for them, and re-layouts, body(): return jnp.stack([col_real * wiener, col_imag * wiener])  25 us
  transfers between devices with their start and end apart: 5, of which 2 were waited for; matrix products, arithmetic and copies ran while one was open for 4% of the time, Pallas kernels for 0%

commit v1 on v0

v1 whole, which is shorter than its diff:
```python
import functools
import math

import jax
import jax.numpy as jnp
from jax import lax
from jax.experimental import pallas as pl
from jax.experimental.pallas import tpu as pltpu
from jax.sharding import PartitionSpec as P

PIECE = 16
LANES = 128
LOW = 16
HIGH = LANES // LOW
ROWS = 2048
COLS = 4096
SCALE = 1.0 / math.sqrt(ROWS * COLS)
GROUP = 16
F32 = jnp.float32
BF16 = jnp.bfloat16
NT = (((1,), (1,)), ((), ()))


def iota(shape, dim):
    return lax.broadcasted_iota(jnp.int32, shape, dim)


def turn(m, modulus):
    quarter = modulus // 4
    quadrant = (m + quarter // 2) // quarter if quarter & (quarter - 1) else (
        lax.shift_right_logical(m + quarter // 2, int(math.log2(quarter))))
    x = (m - quadrant * quarter).astype(F32) * (2.0 * math.pi / modulus)
    y = x * x
    s = x + x * y * (-1.0 / 6 + y * (1.0 / 120 + y * (-1.0 / 5040 + y * (1.0 / 362880))))
    c = 1.0 + y * (-0.5 + y * (1.0 / 24 + y * (-1.0 / 720 + y * (1.0 / 40320))))
    swap = (quadrant & 1) == 1
    cos = jnp.where(swap, s, c)
    sin = jnp.where(swap, c, s)
    cos = jnp.where(((quadrant + 1) & 2) == 2, -cos, cos)
    sin = jnp.where((quadrant & 2) == 2, -sin, sin)
    return cos, sin


def halves(value):
    high = value.astype(BF16)
    return high, (value - high.astype(F32)).astype(BF16)


def column(row):
    return jnp.transpose(jnp.broadcast_to(row, (LANES, LANES)))


def bin_kernel(
    rows_own, col_blocks,
    own_ref, before_ref, after_ref, taps_ref, plate_ref, angle_ref, weight_ref, pixel_ref, owner_ref, block_ref,
    out_ref,
    window, stokes, high_ref, low_ref, left, right,
):
    samples, dets = own_ref.shape
    groups = dets // LANES
    reach = before_ref.shape[0]
    window[:reach] = before_ref[...]
    window[reach : reach + samples] = own_ref[...]
    window[reach + samples :] = after_ref[...]
    width = taps_ref.shape[1]
    band = pltpu.roll(
        jnp.broadcast_to(taps_ref[...], (LANES, width)), 0, axis=1, stride=1, stride_axis=0
    ).astype(BF16)
    twice = 2.0 * angle_ref[...]
    cos_det, sin_det = jnp.cos(twice), jnp.sin(twice)
    quad = 4.0 * plate_ref[...]
    cos_plate, sin_plate = jnp.cos(quad), jnp.sin(quad)
    for part in range(samples // LANES):
        span = slice(part * LANES, (part + 1) * LANES)
        filtered = jnp.dot(
            band, window[part * LANES : part * LANES + width, :], preferred_element_type=F32
        )
        weighted = filtered * weight_ref[...]
        cos_p = jnp.concatenate([column(cos_plate[part : part + 1])] * groups, axis=1)
        sin_p = jnp.concatenate([column(sin_plate[part : part + 1])] * groups, axis=1)
        stokes[0, span] = weighted.astype(BF16).astype(F32)
        stokes[1, span] = (weighted * (cos_p * cos_det - sin_p * sin_det)).astype(BF16).astype(F32)
        stokes[2, span] = (weighted * (sin_p * cos_det + cos_p * sin_det)).astype(BF16).astype(F32)
    pixels = pixel_ref[...]
    high_ref[...] = lax.shift_right_logical(pixels, int(math.log2(LOW)))
    low_ref[...] = pixels & (LOW - 1)
    high_ids = iota((HIGH, dets), 0)
    low_ids = iota((LOW, dets), 0)
    pieces = GROUP // groups

    def group_step(g, carry):
        def piece_step(p, inner):
            first = (g * pieces + p) * PIECE
            for t in range(PIECE):
                row = pl.ds(first + t, 1)
                lanes = slice(t * LANES, (t + 1) * LANES)
                hot = jnp.broadcast_to(high_ref[row, :], (HIGH, dets)) == high_ids
                for s in range(3):
                    spread = jnp.where(hot, jnp.broadcast_to(stokes[s, row, :], (HIGH, dets)), 0.0)
                    both = jnp.concatenate(
                        [spread[:, k * LANES : (k + 1) * LANES] for k in range(groups)], axis=0
                    )
                    at = pl.multiple_of(p * (groups * HIGH), groups * HIGH)
                    left[s, pl.ds(at, groups * HIGH), lanes] = both.astype(BF16)
                low = jnp.where(
                    jnp.broadcast_to(low_ref[row, :], (LOW, dets)) == low_ids, 1.0, 0.0
                ).astype(BF16)
                for k in range(groups):
                    at = pl.multiple_of((p * groups + k) * LOW, LOW)
                    right[pl.ds(at, LOW), lanes] = low[:, k * LANES : (k + 1) * LANES]
            return inner

        lax.fori_loop(0, pieces, piece_step, 0)
        for s in range(3):
            sums = lax.dot_general(left[s], right[...], NT, preferred_element_type=F32)
            mine = lax.div(iota((HIGH, LANES), 1), LOW) == iota((HIGH, LANES), 0)
            rows = []
            for i in range(GROUP):
                start = (i * LOW) // LANES * LANES
                part = sums[i * HIGH : (i + 1) * HIGH, start : start + LANES]
                if start != i * LOW:
                    part = pltpu.roll(part, (start - i * LOW) % LANES, axis=1)
                part = pltpu.roll(part, 0, axis=1, stride=LOW, stride_axis=0)
                rows.append(jnp.sum(jnp.where(mine, part, 0.0), axis=0, keepdims=True))
            out_ref[pl.ds(pl.multiple_of(g * GROUP, GROUP), GROUP), s * LANES : (s + 1) * LANES] = (
                jnp.concatenate(rows, axis=0)
            )
        return carry

    tiles = owner_ref.shape[1]
    lax.fori_loop(0, tiles // GROUP, group_step, 0)
    block = block_ref[...]
    shift = int(math.log2(col_blocks))
    map_row = owner_ref[...] * rows_own + lax.shift_right_logical(block, shift)
    map_col = block & (col_blocks - 1)
    out_ref[tiles:] = jnp.zeros_like(out_ref[tiles:])
    for k, index in ((0, map_row), (1, map_col)):
        twin = jnp.concatenate([index, index], axis=1).astype(F32)
        out_ref[tiles + k : tiles + k + 1, : 2 * tiles] = twin


def spectrum_kernel(
    count, chunks, parts, passes,
    first_ref, mine_ref, other_ref, wiener_ref,
    out_ref,
    tiles, turns, cosine, sine, phase_cos, phase_sin, total,
):
    step = pl.program_id(0) * pl.num_programs(1) + pl.program_id(1)
    chunk = pl.program_id(2)
    kx_block = wiener_ref.shape[1]
    width = parts * LANES
    half = ROWS // 2
    held = LANES // 2
    repeat = phase_cos.shape[0]

    @pl.when(step == 0)
    def _():
        for at in range(0, count, LANES):
            size = min(LANES, count - at)
            kx = first_ref[0] + at + iota((size, LANES), 0)
            c, s = turn((kx * iota((size, LANES), 1)) & (COLS - 1), COLS)
            c, s = c * SCALE, s * SCALE
            high, low = halves(c)
            turns[0, at : at + size, :LANES] = high
            turns[0, at : at + size, LANES:] = low
            high, low = halves(-s)
            turns[1, at : at + size, :LANES] = high
            turns[1, at : at + size, LANES:] = low

    def build():
        left_side = iota((1, LANES), 1) < held
        for p in range(parts):
            rows = slice(p * LANES, (p + 1) * LANES)
            tiles[p * LANES : p * LANES + held] = mine_ref[p, :held]
            tiles[p * LANES + held : (p + 1) * LANES] = other_ref[p, :held]
            r = jnp.where(left_side, mine_ref[p, held : held + 1, :LANES], other_ref[p, held : held + 1, :LANES])
            b = jnp.where(left_side, mine_ref[p, held + 1 : held + 2, :LANES], other_ref[p, held + 1 : held + 2, :LANES])
            ri, bi = r.astype(jnp.int32), b.astype(jnp.int32)
            kx = first_ref[0] + iota((repeat, LANES), 0)
            c, s = turn((ri - kx * bi * LANES) & (2 * ROWS - 1), 2 * ROWS)
            phase_cos[:, rows] = c
            phase_sin[:, rows] = s
            down = column(r).astype(jnp.int32)
            c, s = turn((down * (2 * iota((LANES, LANES), 1) + 1)) & (2 * ROWS - 1), 2 * ROWS)
            cs, ss = turn((down * (2 * LANES)) & (2 * ROWS - 1), 2 * ROWS)
            for at in range(0, half, LANES):
                cosine[rows, at : at + LANES] = c.astype(BF16)
                sine[rows, at : at + LANES] = s.astype(BF16)
                c, s = c * cs - s * ss, c * ss + s * cs

    if chunks == 1:
        pl.when(step == 0)(build)
    else:
        build()

    stokes = pl.program_id(0)
    data = tiles[:, pl.ds(pl.multiple_of(stokes * LANES, LANES), LANES)]
    high, low = halves(data)
    twice = jnp.concatenate([high, high], axis=1)
    at = pl.multiple_of(pl.program_id(1) * kx_block, kx_block)

    def columns(k):
        table = turns[k, pl.ds(at, kx_block), :]
        y = lax.dot_general(table, twice, NT, preferred_element_type=F32)
        return y + lax.dot_general(table[:, :LANES], low, NT, preferred_element_type=F32)

    real, imag = columns(0), columns(1)
    pc = jnp.concatenate([phase_cos[...]] * (kx_block // repeat), axis=0)
    ps = jnp.concatenate([phase_sin[...]] * (kx_block // repeat), axis=0)
    rows = jnp.concatenate([real * pc - imag * ps, real * ps + imag * pc], axis=0)
    split = halves(rows) if passes == 2 else (rows.astype(BF16),)
    chunk_width = 2 * LANES
    flip = LANES - 1 - iota((kx_block, LANES), 1)

    def reverse(value):
        pieces = [
            jnp.take_along_axis(value[:, k : k + LANES], flip, axis=1)
            for k in range(0, value.shape[1], LANES)
        ]
        return jnp.concatenate(pieces[::-1], axis=1)

    for n in range(0, half, chunk_width):
        lanes = slice(n, n + chunk_width)
        back = slice(ROWS - n - chunk_width, ROWS - n)
        even = sum(jnp.dot(part, cosine[:, lanes], preferred_element_type=F32) for part in split)
        odd = sum(jnp.dot(part, sine[:, lanes], preferred_element_type=F32) for part in split)
        re_even, im_even = even[:kx_block], even[kx_block:]
        re_odd, im_odd = odd[:kx_block], odd[kx_block:]
        values = (
            (0, lanes, re_even + im_odd), (1, lanes, im_even - re_odd),
            (0, back, reverse(re_even - im_odd)), (1, back, reverse(im_even + re_odd)),
        )
        for k, where, value in values:
            if chunks == 1:
                out_ref[k, 0, :, where] = value * wiener_ref[0, :, where]
            else:
                @pl.when(chunk == 0)
                def _():
                    total[k, :, where] = value

                @pl.when(chunk > 0)
                def _():
                    total[k, :, where] += value

    if chunks > 1:
        @pl.when(chunk == chunks - 1)
        def _():
            for k in range(2):
                out_ref[k, 0] = total[k] * wiener_ref[0]


def neighbours(value, axis):
    size = lax.axis_size(axis)
    up = [(i, i + 1) for i in range(size - 1)]
    return lax.ppermute(value, axis, up), lax.ppermute(value, axis, [(j, i) for i, j in up])


def gather(value, axis):
    size = lax.axis_size(axis)
    if size // 2 > 8:
        whole = lax.all_gather(value, axis, axis=0)
        return whole[: size // 2], whole[size // 2 :]
    found = [value] + [
        lax.ppermute(value, axis, [(i, (i + 2 * k) % size) for i in range(size)])
        for k in range(1, size // 2)
    ]
    mine = jnp.stack(found)
    return mine, lax.ppermute(mine, axis, [(i, i ^ 1) for i in range(size)])


def body(
    timeline, pointing, plate_angle, detector_angle, detector_weight, kernel, tile_owner, tile_block, wiener
):
    samples, dets = timeline.shape
    tiles = tile_owner.shape[0]
    devices = lax.axis_size("tm")
    before, after = neighbours(timeline, "tm")
    count_taps = kernel.shape[0]
    reach = (count_taps - 1) // 2
    before, after = before[samples - reach :], after[:reach]
    width = count_taps - 1 + LANES
    taps = jnp.pad(kernel.astype(F32), (0, width - count_taps)).reshape(1, width)
    plate = jnp.pad(plate_angle.reshape(samples // LANES, LANES), ((0, 8 - samples // LANES), (0, 0)))
    rows_own = ROWS // devices
    col_blocks = COLS // LANES
    packed = pl.pallas_call(
        functools.partial(bin_kernel, rows_own, col_blocks),
        out_shape=jax.ShapeDtypeStruct((tiles + 8, 3 * LANES), F32),
        scratch_shapes=[
            pltpu.VMEM((2 * reach + samples, dets), BF16),
            pltpu.VMEM((3, samples, dets), F32),
            pltpu.VMEM((samples, dets), jnp.int32),
            pltpu.VMEM((samples, dets), jnp.int32),
            pltpu.VMEM((3, GROUP * HIGH, PIECE * LANES), BF16),
            pltpu.VMEM((GROUP * LOW, PIECE * LANES), BF16),
        ],
        name="bin_tiles",
    )(
        timeline, before, after, taps, plate, detector_angle.reshape(1, dets), detector_weight.reshape(1, dets),
        pointing, tile_owner.reshape(1, tiles), tile_block.reshape(1, tiles),
    )
    mine, other = gather(packed, "tm")
    stokes, count, ky = wiener.shape
    total_parts = mine.shape[0]
    parts = min(4, total_parts)
    chunks = total_parts // parts
    kx_block = min(128, count)
    repeat = min(COLS // LANES, kx_block)
    passes = 2
    first = (lax.axis_index("tm") * count).astype(jnp.int32).reshape(1)
    piece = pl.BlockSpec((parts, tiles + 8, 3 * LANES), lambda s, k, c, _: (c, 0, 0))
    return pl.pallas_call(
        functools.partial(spectrum_kernel, count, chunks, parts, passes),
        grid_spec=pltpu.PrefetchScalarGridSpec(
            num_scalar_prefetch=1,
            grid=(stokes, count // kx_block, chunks),
            in_specs=[piece, piece, pl.BlockSpec((1, kx_block, ky), lambda s, k, c, _: (s, k, 0))],
            out_specs=pl.BlockSpec((2, 1, kx_block, ky), lambda s, k, c, _: (0, s, k, 0)),
            scratch_shapes=[
                pltpu.VMEM((parts * LANES, 3 * LANES), F32),
                pltpu.VMEM((2, count, 2 * LANES), BF16),
                pltpu.VMEM((parts * LANES, ROWS // 2), BF16),
                pltpu.VMEM((parts * LANES, ROWS // 2), BF16),
                pltpu.VMEM((repeat, parts * LANES), F32),
                pltpu.VMEM((repeat, parts * LANES), F32),
                pltpu.VMEM((2, kx_block, ky) if chunks > 1 else (8, LANES), F32),
            ],
        ),
        out_shape=jax.ShapeDtypeStruct((2, stokes, count, ky), F32),
        name="spectra",
    )(first, mine, other, wiener)


def solution(mesh):
    placed = (
        P("tm", "band"), P("tm", "band"), P("tm"), P("band"), P("band"), P("band"),
        P("tm", "band"), P("tm", "band"), P("band", "tm", None),
    )
    return jax.shard_map(
        body, mesh=mesh, in_specs=placed, out_specs=P(None, "band", "tm", None), check_vma=False
    )
```

time: 1240 us -> 68.9 us (0.06)
  waiting for transfers between devices: 538 us -> 13.4 us
  matrix products: 379 us -> 0 us
  local copies, waits for them, and re-layouts: 224 us -> 3.34 us
  other arithmetic: 65.2 us -> 1.63 us
  Pallas kernels: 0 us -> 38.4 us
  starting transfers between devices: 24 us -> 11.4 us
    all_to_all x3 -> x0, waiting for transfers between devices: 538 us -> none  [the longest x1 531 us: body(): lax.all_to_all(jnp.stack([row_real, row_imag]), 'tm', split_axis=3, conca...]
    dot_general x26 -> x0, matrix products: 379 us -> none  [the longest x14 356 us: contract(): jnp.einsum(spec_text, left_side, right_side, precision=lax.Precision.HIGH...]
    another operation x10 -> x0, local copies, waits for them, and re-layouts: 70.3 us -> none  [the longest x1 42 us: body(): jnp.stack([row_real, row_imag])]
    mul x20 -> x0, local copies, waits for them, and re-layouts: 65.9 us -> none  [the longest x2 32.8 us: fourier_last(): imag_out.reshape(leading + (length,)) * factor]
    all_to_all x4 -> x0, local copies, waits for them, and re-layouts: 44.5 us -> none  [the longest x2 43.8 us: body(): lax.all_to_all(jnp.stack([row_real, row_imag]), 'tm', split_axis=3, conca...]
    pallas_call x0 -> x2, Pallas kernels: none -> 38.4 us  [the longest x1 27.5 us: body(): pl.pallas_call(functools.partial(spectrum_kernel, count, chunks, parts, p...]
    another operation x3 -> x1, other arithmetic: 31.4 us -> 0.93 us  [gather(): mine = jnp.stack(found)]
    all_to_all x3 -> x0, starting transfers between devices: 19.5 us -> none  [the longest x1 7.55 us: body(): lax.all_to_all(labels, 'tm', split_axis=0, concat_axis=0, tiled=True)]
  transfers between devices with their start and end apart: 5 -> 6, of which waited for: 2 -> 4; matrix products, arithmetic and copies ran while one was open for 4% -> 4% of each run, Pallas kernels for 0% -> 0%
where the time goes in v1:
time: 68.9 us; the launch traced here: 68.2 us
  Pallas kernels  38.4 us (56%)
  waiting for transfers between devices  13.4 us (19%)
  starting transfers between devices  11.4 us (17%)
  local copies, waits for them, and re-layouts  3.34 us (5%)
  other arithmetic  1.63 us (2%)
    pallas_call x1, Pallas kernels, body(): pl.pallas_call(functools.partial(spectrum_kernel, count, chunks, parts, p...  27.5 us
    pallas_call x1, Pallas kernels, body(): pl.pallas_call(functools.partial(bin_kernel, rows_own, col_blocks), out_s...  10.9 us
    ppermute x3, waiting for transfers between devices, gather(): lax.ppermute(value, axis, [(i, (i + 2 * k) % size) for i in range(size)])  9.65 us
    ppermute x3, starting transfers between devices, gather(): lax.ppermute(value, axis, [(i, (i + 2 * k) % size) for i in range(size)])  7.62 us
    ppermute x1, starting transfers between devices, neighbours(): lax.ppermute(value, axis, up)  2.4 us
    ppermute x1, waiting for transfers between devices, neighbours(): lax.ppermute(value, axis, [(j, i) for i, j in up])  1.94 us
    ppermute x1, waiting for transfers between devices, gather(): return (mine, lax.ppermute(mine, axis, [(i, i ^ 1) for i in range(size)]))  1.78 us
    unnamed x8, local copies, waits for them, and re-layouts  1.47 us
  transfers between devices with their start and end apart: 6, of which 4 were waited for; matrix products, arithmetic and copies ran while one was open for 4% of the time, Pallas kernels for 0%

profile of v1, /device:TPU:0, one launch (start us, length us, event | category | flops | bytes accessed | tf_op | source)
XLA Modules:
  0.0 68.2 jit_solution(14803944688389819209)
XLA Ops:
  0.0 2.4 %collective-permute-start = (bf16[512,256]{1,0:T(8,128)(2,1)}, bf16[512,256]{1,0:T(8,128)(2,1)S(1)}, u32[]{:S(2)}, u32[]{:S(2)}) collective-permute-start(bf16[512,256]{1,0:T(8,128)(2,1)} %own_ref.1), channel_id=1, source_target_pairs={{0,1},{1,2},{2,3},{3,4},{4,5},{5,6},{6,7},{8,9},{9,10},{10,11},{11... | collective-permute-start | bytes 786440 | tf_op jit(solution)/shard_map/ppermute | solution.py:255
  2.4 1.3 %collective-permute-start.1 = (bf16[512,256]{1,0:T(8,128)(2,1)}, bf16[512,256]{1,0:T(8,128)(2,1)S(1)}, u32[]{:S(2)}, u32[]{:S(2)}) collective-permute-start(bf16[512,256]{1,0:T(8,128)(2,1)} %own_ref.1), channel_id=1, source_target_pairs={{1,0},{2,1},{3,2},{4,3},{5,4},{6,5},{7,6},{9,8},{10,9},{11,10},{12... | collective-permute-start | bytes 786440 | tf_op jit(solution)/shard_map/ppermute | solution.py:255
  3.7 0.7 %pad_convert_fusion = f32[1152]{0:T(1024)S(1)} fusion(bf16[1025]{0:T(1024)(128)(2,1)} %param.14), kind=kLoop, calls=%fused_computation.1 | loop fusion | flops 1152 | bytes 6658 | tf_op jit(solution)/shard_map/reshape | solution.py:282
  4.4 0.6 reshape.32.taps_ref
  5.0 1.3 %pad.10.plate_ref = f32[8,128]{1,0:T(8,128)} pad(f32[4,128]{1,0:T(4,128)} %bitcast.14, f32[]{:T(128)} %constant.10.clone.1), padding=0_4x0_0 | pad | bytes 6148 | tf_op jit(solution)/shard_map/jit(_pad)/pad | solution.py:283
  6.3 0.0 collective-permute-done.before_ref
  6.3 0.0 copy-start.2
  6.3 1.9 %collective-permute-done.1.after_ref = bf16[512,256]{1,0:T(8,128)(2,1)S(1)} collective-permute-done((bf16[512,256]{1,0:T(8,128)(2,1)}, bf16[512,256]{1,0:T(8,128)(2,1)S(1)}, u32[]{:S(2)}, u32[]{:S(2)}) %collective-permute-start.1) | collective-permute-done | bytes 262176 | tf_op jit(solution)/shard_map/ppermute | solution.py:255
  8.2 0.0 copy-start.3
  8.2 0.0 copy-done.2
  8.2 0.7 %copy-done.3 = bf16[512,256]{1,0:T(8,128)(2,1)} copy-done((bf16[512,256]{1,0:T(8,128)(2,1)}, bf16[512,256]{1,0:T(8,128)(2,1)S(1)}, u32[]{:S(2)}) %copy-start.3) | copy-done | bytes 262168
  8.9 10.9 %bin_tiles.1 = f32[72,384]{1,0:T(8,128)} custom-call(bf16[512,256]{1,0:T(8,128)(2,1)} %own_ref.1, bf16[512,256]{1,0:T(8,128)(2,1)} %copy-done.2, bf16[512,256]{1,0:T(8,128)(2,1)} %copy-done.3, f32[1,1152]{1,0:T(1,128)} %reshape.32.taps_ref, f32[8,128]{1,0:T(8,128)} %pad.10.plate_ref, f32[1,256]{1,0:T(1,128)} %bitcast.15, f32[1,256]{1,0:T(1,128)} %bitcast.16, ...), custom_call_target="tpu_custom_call" | custom-call | tf_op jit(solution)/shard_map/bin_tiles/pallas_call | solution.py:286
  19.8 6.6 %collective-permute-start.4 = (f32[72,384]{1,0:T(8,128)}, f32[72,384]{1,0:T(8,128)S(1)}, u32[]{:S(2)}, u32[]{:S(2)}) collective-permute-start(f32[72,384]{1,0:T(8,128)} %bin_tiles.1), channel_id=1, source_target_pairs={{0,6},{1,7},{2,0},{3,1},{4,2},{5,3},{6,4},{7,5},{8,14},{9,15},{10,... | collective-permute-start | bytes 331784 | tf_op jit(solution)/shard_map/ppermute | solution.py:264
  26.4 0.0 collective-permute-start.3
  26.4 1.0 %collective-permute-start.2 = (f32[72,384]{1,0:T(8,128)}, f32[72,384]{1,0:T(8,128)S(1)}, u32[]{:S(2)}, u32[]{:S(2)}) collective-permute-start(f32[72,384]{1,0:T(8,128)} %bin_tiles.1), channel_id=1, source_target_pairs={{0,2},{1,3},{2,4},{3,5},{4,6},{5,7},{6,0},{7,1},{8,10},{9,11},{10,... | collective-permute-start | bytes 331784 | tf_op jit(solution)/shard_map/ppermute | solution.py:264
  27.4 2.8 %collective-permute-done.4 = f32[72,384]{1,0:T(8,128)S(1)} collective-permute-done((f32[72,384]{1,0:T(8,128)}, f32[72,384]{1,0:T(8,128)S(1)}, u32[]{:S(2)}, u32[]{:S(2)}) %collective-permute-start.4) | collective-permute-done | bytes 110624 | tf_op jit(solution)/shard_map/ppermute | solution.py:264
  30.3 6.8 %collective-permute-done.3 = f32[72,384]{1,0:T(8,128)S(1)} collective-permute-done((f32[72,384]{1,0:T(8,128)}, f32[72,384]{1,0:T(8,128)S(1)}, u32[]{:S(2)}, u32[]{:S(2)}) %collective-permute-start.3) | collective-permute-done | bytes 110624 | tf_op jit(solution)/shard_map/ppermute | solution.py:264
  37.1 0.0 collective-permute-done.2
  37.1 0.9 %pad_maximum_fusion.mine_ref = f32[4,72,384]{2,1,0:T(8,128)S(1)} fusion(f32[1,72,384]{2,1,0:T(8,128)S(1)} %bitcast.11, f32[1,72,384]{2,1,0:T(8,128)S(1)} %bitcast.12, f32[1,72,384]{2,1,0:T(8,128)S(1)} %bitcast.13, f32[1,72,384]{2,1,0:T(8,128)} %bitcast.10), kind=kLoop, calls=%fused_computation | loop fusion | flops 331776 | bytes 884736 | tf_op jit(solution)/shard_map/stack | solution.py:267
  38.0 0.0 copy-start
  38.0 0.1 collective-permute-start.5
  38.1 1.8 %collective-permute-done.5.other_ref = f32[4,72,384]{2,1,0:T(8,128)S(1)} collective-permute-done((f32[4,72,384]{2,1,0:T(8,128)S(1)}, f32[4,72,384]{2,1,0:T(8,128)S(1)}, u32[]{:S(2)}, u32[]{:S(2)}) %collective-permute-start.5) | collective-permute-done | bytes 442400 | tf_op jit(solution)/shard_map/ppermute | solution.py:268
  39.9 0.0 copy-start.1
  39.9 0.0 copy-done
  39.9 0.8 %copy-done.1 = f32[4,72,384]{2,1,0:T(8,128)} copy-done((f32[4,72,384]{2,1,0:T(8,128)}, f32[4,72,384]{2,1,0:T(8,128)S(1)}, u32[]{:S(2)}) %copy-start.1) | copy-done | bytes 442392
  40.7 27.5 %spectra.1 = f32[2,3,512,2048]{3,2,1,0:T(8,128)} custom-call(s32[1]{0:T(128)} %bitcast.first_ref, f32[4,72,384]{2,1,0:T(8,128)} %copy-done, f32[4,72,384]{2,1,0:T(8,128)} %copy-done.1, f32[3,512,2048]{2,1,0:T(8,128)} %wiener_ref.1), custom_call_target="tpu_custom_call" | custom-call | tf_op jit(solution)/shard_map/spectra/pallas_call | solution.py:312
Async XLA Ops:
  0.0 6.3 %collective-permute-start = (bf16[512,256]{1,0:T(8,128)(2,1)}, bf16[512,256]{1,0:T(8,128)(2,1)S(1)}, u32[]{:S(2)}, u32[]{:S(2)}) collective-permute-start(bf16[512,256]{1,0:T(8,128)(2,1)} %own_ref.1), channel_id=1, source_target_pairs={{0,1},{1,2},{2,3},{3,4},{4,5},{5,6},{6,7},{8,9},{9,10},{10,11},{11... | collective-permute-start | bytes 786440 | tf_op jit(solution)/shard_map/ppermute | solution.py:255
  2.4 5.8 %collective-permute-start.1 = (bf16[512,256]{1,0:T(8,128)(2,1)}, bf16[512,256]{1,0:T(8,128)(2,1)S(1)}, u32[]{:S(2)}, u32[]{:S(2)}) collective-permute-start(bf16[512,256]{1,0:T(8,128)(2,1)} %own_ref.1), channel_id=1, source_target_pairs={{1,0},{2,1},{3,2},{4,3},{5,4},{6,5},{7,6},{9,8},{10,9},{11,10},{12... | collective-permute-start | bytes 786440 | tf_op jit(solution)/shard_map/ppermute | solution.py:255
  6.3 1.9 %copy-start.2 = (bf16[512,256]{1,0:T(8,128)(2,1)}, bf16[512,256]{1,0:T(8,128)(2,1)S(1)}, u32[]{:S(2)}) copy-start(bf16[512,256]{1,0:T(8,128)(2,1)S(1)} %collective-permute-done.before_ref) | copy-start | bytes 786436
  8.2 0.7 %copy-start.3 = (bf16[512,256]{1,0:T(8,128)(2,1)}, bf16[512,256]{1,0:T(8,128)(2,1)S(1)}, u32[]{:S(2)}) copy-start(bf16[512,256]{1,0:T(8,128)(2,1)S(1)} %collective-permute-done.1.after_ref) | copy-start | bytes 786436
  19.8 10.4 %collective-permute-start.4 = (f32[72,384]{1,0:T(8,128)}, f32[72,384]{1,0:T(8,128)S(1)}, u32[]{:S(2)}, u32[]{:S(2)}) collective-permute-start(f32[72,384]{1,0:T(8,128)} %bin_tiles.1), channel_id=1, source_target_pairs={{0,6},{1,7},{2,0},{3,1},{4,2},{5,3},{6,4},{7,5},{8,14},{9,15},{10,... | collective-permute-start | bytes 331784 | tf_op jit(solution)/shard_map/ppermute | solution.py:264
  26.4 10.7 %collective-permute-start.3 = (f32[72,384]{1,0:T(8,128)}, f32[72,384]{1,0:T(8,128)S(1)}, u32[]{:S(2)}, u32[]{:S(2)}) collective-permute-start(f32[72,384]{1,0:T(8,128)} %bin_tiles.1), channel_id=1, source_target_pairs={{0,4},{1,5},{2,6},{3,7},{4,0},{5,1},{6,2},{7,3},{8,12},{9,13},{10,... | collective-permute-start | bytes 331784 | tf_op jit(solution)/shard_map/ppermute | solution.py:264
  26.4 10.7 %collective-permute-start.2 = (f32[72,384]{1,0:T(8,128)}, f32[72,384]{1,0:T(8,128)S(1)}, u32[]{:S(2)}, u32[]{:S(2)}) collective-permute-start(f32[72,384]{1,0:T(8,128)} %bin_tiles.1), channel_id=1, source_target_pairs={{0,2},{1,3},{2,4},{3,5},{4,6},{5,7},{6,0},{7,1},{8,10},{9,11},{10,... | collective-permute-start | bytes 331784 | tf_op jit(solution)/shard_map/ppermute | solution.py:264
  38.0 1.9 %copy-start = (f32[4,72,384]{2,1,0:T(8,128)}, f32[4,72,384]{2,1,0:T(8,128)S(1)}, u32[]{:S(2)}) copy-start(f32[4,72,384]{2,1,0:T(8,128)S(1)} %pad_maximum_fusion.mine_ref) | copy-start | bytes 1327108
  38.0 1.9 %collective-permute-start.5 = (f32[4,72,384]{2,1,0:T(8,128)S(1)}, f32[4,72,384]{2,1,0:T(8,128)S(1)}, u32[]{:S(2)}, u32[]{:S(2)}) collective-permute-start(f32[4,72,384]{2,1,0:T(8,128)S(1)} %pad_maximum_fusion.mine_ref), channel_id=1, source_target_pairs={{0,1},{1,0},{2,3},{3,2},{4,5},{5,4},{6,7},{7,6},{8,9},{9,8},{10,11... | collective-permute-start | bytes 1327112 | tf_op jit(solution)/shard_map/ppermute | solution.py:268
  39.9 0.8 %copy-start.1 = (f32[4,72,384]{2,1,0:T(8,128)}, f32[4,72,384]{2,1,0:T(8,128)S(1)}, u32[]{:S(2)}) copy-start(f32[4,72,384]{2,1,0:T(8,128)S(1)} %collective-permute-done.5.other_ref) | copy-start | bytes 1327108

commit v2 on v1

--- a/solution.py
+++ b/solution.py
@@ -139,114 +139,131 @@
         out_ref[tiles + k : tiles + k + 1, : 2 * tiles] = twin
 
 
+def table_kernel(first_ref, wiener_ref, ready_ref, held_ref, turns_ref, sem):
+    del ready_ref
+    copy = pltpu.make_async_copy(wiener_ref, held_ref, sem)
+    copy.start()
+    count = turns_ref.shape[1]
+    for at in range(0, count, LANES):
+        size = min(LANES, count - at)
+        kx = first_ref[0] + at + iota((size, LANES), 0)
+        c, s = turn((kx * iota((size, LANES), 1)) & (COLS - 1), COLS)
+        for k, value in enumerate((c * SCALE, s * -SCALE)):
+            high, low = halves(value)
+            turns_ref[k, at : at + size, :LANES] = high
+            turns_ref[k, at : at + size, LANES:] = low
+    copy.wait()
+
+
 def spectrum_kernel(
-    count, chunks, parts, passes,
-    first_ref, mine_ref, other_ref, wiener_ref,
+    first_ref, mine_ref, other_ref, wiener_ref, turns_ref,
     out_ref,
-    tiles, turns, cosine, sine, phase_cos, phase_sin, total,
+    tiles, factor, table, base, advance, phases, buffer, sems,
 ):
-    step = pl.program_id(0) * pl.num_programs(1) + pl.program_id(1)
-    chunk = pl.program_id(2)
-    kx_block = wiener_ref.shape[1]
-    width = parts * LANES
-    half = ROWS // 2
+    parts = mine_ref.shape[0]
+    stokes, count, ky = wiener_ref.shape
     held = LANES // 2
-    repeat = phase_cos.shape[0]
-
-    @pl.when(step == 0)
-    def _():
-        for at in range(0, count, LANES):
-            size = min(LANES, count - at)
-            kx = first_ref[0] + at + iota((size, LANES), 0)
-            c, s = turn((kx * iota((size, LANES), 1)) & (COLS - 1), COLS)
-            c, s = c * SCALE, s * SCALE
-            high, low = halves(c)
-            turns[0, at : at + size, :LANES] = high
-            turns[0, at : at + size, LANES:] = low
-            high, low = halves(-s)
-            turns[1, at : at + size, :LANES] = high
-            turns[1, at : at + size, LANES:] = low
-
-    def build():
-        left_side = iota((1, LANES), 1) < held
-        for p in range(parts):
-            rows = slice(p * LANES, (p + 1) * LANES)
-            tiles[p * LANES : p * LANES + held] = mine_ref[p, :held]
-            tiles[p * LANES + held : (p + 1) * LANES] = other_ref[p, :held]
-            r = jnp.where(left_side, mine_ref[p, held : held + 1, :LANES], other_ref[p, held : held + 1, :LANES])
-            b = jnp.where(left_side, mine_ref[p, held + 1 : held + 2, :LANES], other_ref[p, held + 1 : held + 2, :LANES])
-            ri, bi = r.astype(jnp.int32), b.astype(jnp.int32)
-            kx = first_ref[0] + iota((repeat, LANES), 0)
-            c, s = turn((ri - kx * bi * LANES) & (2 * ROWS - 1), 2 * ROWS)
-            phase_cos[:, rows] = c
-            phase_sin[:, rows] = s
-            down = column(r).astype(jnp.int32)
-            c, s = turn((down * (2 * iota((LANES, LANES), 1) + 1)) & (2 * ROWS - 1), 2 * ROWS)
-            cs, ss = turn((down * (2 * LANES)) & (2 * ROWS - 1), 2 * ROWS)
-            for at in range(0, half, LANES):
-                cosine[rows, at : at + LANES] = c.astype(BF16)
-                sine[rows, at : at + LANES] = s.astype(BF16)
-                c, s = c * cs - s * ss, c * ss + s * cs
-
-    if chunks == 1:
-        pl.when(step == 0)(build)
-    else:
-        build()
-
-    stokes = pl.program_id(0)
-    data = tiles[:, pl.ds(pl.multiple_of(stokes * LANES, LANES), LANES)]
-    high, low = halves(data)
-    twice = jnp.concatenate([high, high], axis=1)
-    at = pl.multiple_of(pl.program_id(1) * kx_block, kx_block)
-
-    def columns(k):
-        table = turns[k, pl.ds(at, kx_block), :]
-        y = lax.dot_general(table, twice, NT, preferred_element_type=F32)
-        return y + lax.dot_general(table[:, :LANES], low, NT, preferred_element_type=F32)
-
-    real, imag = columns(0), columns(1)
-    pc = jnp.concatenate([phase_cos[...]] * (kx_block // repeat), axis=0)
-    ps = jnp.concatenate([phase_sin[...]] * (kx_block // repeat), axis=0)
-    rows = jnp.concatenate([real * pc - imag * ps, real * ps + imag * pc], axis=0)
-    split = halves(rows) if passes == 2 else (rows.astype(BF16),)
-    chunk_width = 2 * LANES
-    flip = LANES - 1 - iota((kx_block, LANES), 1)
-
-    def reverse(value):
-        pieces = [
-            jnp.take_along_axis(value[:, k : k + LANES], flip, axis=1)
-            for k in range(0, value.shape[1], LANES)
-        ]
-        return jnp.concatenate(pieces[::-1], axis=1)
-
-    for n in range(0, half, chunk_width):
-        lanes = slice(n, n + chunk_width)
-        back = slice(ROWS - n - chunk_width, ROWS - n)
-        even = sum(jnp.dot(part, cosine[:, lanes], preferred_element_type=F32) for part in split)
-        odd = sum(jnp.dot(part, sine[:, lanes], preferred_element_type=F32) for part in split)
-        re_even, im_even = even[:kx_block], even[kx_block:]
-        re_odd, im_odd = odd[:kx_block], odd[kx_block:]
-        values = (
-            (0, lanes, re_even + im_odd), (1, lanes, im_even - re_odd),
-            (0, back, reverse(re_even - im_odd)), (1, back, reverse(im_even + re_odd)),
-        )
-        for k, where, value in values:
-            if chunks == 1:
-                out_ref[k, 0, :, where] = value * wiener_ref[0, :, where]
-            else:
-                @pl.when(chunk == 0)
-                def _():
-                    total[k, :, where] = value
-
-                @pl.when(chunk > 0)
-                def _():
-                    total[k, :, where] += value
-
-    if chunks > 1:
-        @pl.when(chunk == chunks - 1)
+    repeat = phases.shape[1]
+    block = min(256, count)
+    left_side = iota((1, LANES), 1) < held
+    half_turns = 2 * ROWS - 1
+
+    def build(p, carry):
+        rows = pl.ds(pl.multiple_of(p * LANES, LANES), LANES)
+        low, high = mine_ref.at[p], other_ref.at[p]
+        tiles[pl.ds(pl.multiple_of(p * LANES, LANES), held)] = low[:held]
+        tiles[pl.ds(pl.multiple_of(p * LANES + held, held), held)] = high[:held]
+        r = jnp.where(left_side, low[held : held + 1, :LANES], high[held : held + 1, :LANES])
+        b = jnp.where(left_side, low[held + 1 : held + 2, :LANES], high[held + 1 : held + 2, :LANES])
+        kx = first_ref[0] + iota((repeat, LANES), 0)
+        c, s = turn((r.astype(jnp.int32) - kx * b.astype(jnp.int32) * LANES) & half_turns, 2 * ROWS)
+        phases[0, :, rows] = c
+        phases[1, :, rows] = s
+        down = column(r).astype(jnp.int32)
+        c, s = turn((down * (2 * iota((LANES, LANES), 1) + 1)) & half_turns, 2 * ROWS)
+        base[0, rows] = c
+        base[1, rows] = s
+        c, s = turn((down * (2 * LANES)) & half_turns, 2 * ROWS)
+        advance[0, rows] = c
+        advance[1, rows] = s
+        return carry
+
+    lax.fori_loop(0, parts, build, 0, unroll=parts <= 4)
+    half = ky // 2
+
+    def spread(n, carry):
+        at = pl.ds(pl.multiple_of(n * 2 * LANES, 2 * LANES), LANES)
+        under = pl.ds(pl.multiple_of(n * 2 * LANES + LANES, LANES), LANES)
+        c, s = base[0], base[1]
+        table[:, at] = c.astype(BF16)
+        table[:, under] = s.astype(BF16)
+        base[0] = c * advance[0] - s * advance[1]
+        base[1] = c * advance[1] + s * advance[0]
+        return carry
+
+    lax.fori_loop(0, half // LANES, spread, 0)
+    width = min(4, parts) * LANES
+    flip = LANES - 1 - iota((block, LANES), 1)
+
+    def copies(i, slot):
+        s, k = lax.div(i, count // block), lax.rem(i, count // block)
+        at = pl.ds(pl.multiple_of(k * block, block), block)
+        for side in range(2):
+            yield pltpu.make_async_copy(
+                buffer.at[slot, side], out_ref.at[side, s, at], sems.at[slot, side]
+            )
+
+    def step(i, carry):
+        slot = lax.rem(i, 2)
+        s, k = lax.div(i, count // block), lax.rem(i, count // block)
+        at = pl.ds(pl.multiple_of(k * block, block), block)
+        channel = pl.ds(pl.multiple_of(s * LANES, LANES), LANES)
+
+        def make(q, inner):
+            rows = pl.ds(pl.multiple_of(q * width, width), width)
+            high, low = halves(tiles[rows, channel])
+            twice = jnp.concatenate([high, high], axis=1)
+            real, imag = [
+                lax.dot_general(turns_ref[side, at], twice, NT, preferred_element_type=F32)
+                + lax.dot_general(turns_ref[side, at, :LANES], low, NT, preferred_element_type=F32)
+                for side in range(2)
+            ]
+            pc = jnp.concatenate([phases[0, :, rows]] * (block // repeat), axis=0)
+            ps = jnp.concatenate([phases[1, :, rows]] * (block // repeat), axis=0)
+            factor[:block, rows] = (real * pc - imag * ps).astype(BF16)
+            factor[block:, rows] = (real * ps + imag * pc).astype(BF16)
+            return inner
+
+        lax.fori_loop(0, parts * LANES // width, make, 0)
+
+        @pl.when(i >= 2)
         def _():
-            for k in range(2):
-                out_ref[k, 0] = total[k] * wiener_ref[0]
+            for copy in copies(i, slot):
+                copy.wait()
+
+        for n in range(half // LANES):
+            lanes = slice(n * LANES, (n + 1) * LANES)
+            back = slice(ky - (n + 1) * LANES, ky - n * LANES)
+            both = jnp.dot(
+                factor[...], table[:, 2 * n * LANES : 2 * (n + 1) * LANES], preferred_element_type=F32
+            )
+            re_even, re_odd = both[:block, :LANES], both[:block, LANES:]
+            im_even, im_odd = both[block:, :LANES], both[block:, LANES:]
+            weight = wiener_ref[s, at, lanes]
+            buffer[slot, 0, :, lanes] = (re_even + im_odd) * weight
+            buffer[slot, 1, :, lanes] = (im_even - re_odd) * weight
+            weight = wiener_ref[s, at, back]
+            buffer[slot, 0, :, back] = jnp.take_along_axis(re_even - im_odd, flip, axis=1) * weight
+            buffer[slot, 1, :, back] = jnp.take_along_axis(im_even + re_odd, flip, axis=1) * weight
+        for copy in copies(i, slot):
+            copy.start()
+        return carry
+
+    steps = stokes * (count // block)
+    lax.fori_loop(0, steps, step, 0)
+    for i in (steps - 2, steps - 1):
+        for copy in copies(i, i % 2):
+            copy.wait()
 
 
 def neighbours(value, axis):
@@ -255,16 +272,17 @@
     return lax.ppermute(value, axis, up), lax.ppermute(value, axis, [(j, i) for i, j in up])
 
 
-def gather(value, axis):
+def gather(value, ready, axis):
     size = lax.axis_size(axis)
     if size // 2 > 8:
         whole = lax.all_gather(value, axis, axis=0)
         return whole[: size // 2], whole[size // 2 :]
-    found = [value] + [
+    found = [
         lax.ppermute(value, axis, [(i, (i + 2 * k) % size) for i in range(size)])
         for k in range(1, size // 2)
     ]
-    mine = jnp.stack(found)
+    own, _ = lax.optimization_barrier((value, ready))
+    mine = jnp.stack([own] + found)
     return mine, lax.ppermute(mine, axis, [(i, i ^ 1) for i in range(size)])
 
 
@@ -299,36 +317,49 @@
         timeline, before, after, taps, plate, detector_angle.reshape(1, dets), detector_weight.reshape(1, dets),
         pointing, tile_owner.reshape(1, tiles), tile_block.reshape(1, tiles),
     )
-    mine, other = gather(packed, "tm")
     stokes, count, ky = wiener.shape
-    total_parts = mine.shape[0]
-    parts = min(4, total_parts)
-    chunks = total_parts // parts
-    kx_block = min(128, count)
-    repeat = min(COLS // LANES, kx_block)
-    passes = 2
     first = (lax.axis_index("tm") * count).astype(jnp.int32).reshape(1)
-    piece = pl.BlockSpec((parts, tiles + 8, 3 * LANES), lambda s, k, c, _: (c, 0, 0))
-    return pl.pallas_call(
-        functools.partial(spectrum_kernel, count, chunks, parts, passes),
-        grid_spec=pltpu.PrefetchScalarGridSpec(
-            num_scalar_prefetch=1,
-            grid=(stokes, count // kx_block, chunks),
-            in_specs=[piece, piece, pl.BlockSpec((1, kx_block, ky), lambda s, k, c, _: (s, k, 0))],
-            out_specs=pl.BlockSpec((2, 1, kx_block, ky), lambda s, k, c, _: (0, s, k, 0)),
-            scratch_shapes=[
-                pltpu.VMEM((parts * LANES, 3 * LANES), F32),
-                pltpu.VMEM((2, count, 2 * LANES), BF16),
-                pltpu.VMEM((parts * LANES, ROWS // 2), BF16),
-                pltpu.VMEM((parts * LANES, ROWS // 2), BF16),
-                pltpu.VMEM((repeat, parts * LANES), F32),
-                pltpu.VMEM((repeat, parts * LANES), F32),
-                pltpu.VMEM((2, kx_block, ky) if chunks > 1 else (8, LANES), F32),
-            ],
-        ),
+    vmem, hbm = pl.BlockSpec(memory_space=pltpu.VMEM), pl.BlockSpec(memory_space=pltpu.HBM)
+    scalar = pl.BlockSpec(memory_space=pltpu.SMEM)
+    held, turns = pl.pallas_call(
+        table_kernel,
+        in_specs=[scalar, hbm, pl.BlockSpec(memory_space=pl.ANY)],
+        out_specs=[vmem, vmem],
+        out_shape=[pltpu.VMEM(wiener.shape, F32), pltpu.VMEM((2, count, 2 * LANES), BF16)],
+        scratch_shapes=[pltpu.SemaphoreType.DMA],
+        compiler_params=pltpu.CompilerParams(vmem_limit_bytes=4 * 2**20),
+        cost_estimate=pl.CostEstimate(flops=0, bytes_accessed=2 * wiener.size * 4, transcendentals=0),
+        name="tables",
+    )(first, wiener, packed)
+    mine, other = gather(packed, turns, "tm")
+    parts = min(16, mine.shape[0])
+    block = min(256, count)
+    repeat = min(COLS // LANES, block)
+    every = parts * LANES
+    spectra = pl.pallas_call(
+        spectrum_kernel,
+        in_specs=[scalar, vmem, vmem, vmem, vmem],
+        out_specs=hbm,
+        scratch_shapes=[
+            pltpu.VMEM((every, 3 * LANES), F32),
+            pltpu.VMEM((2 * block, every), BF16),
+            pltpu.VMEM((every, ky), BF16),
+            pltpu.VMEM((2, every, LANES), F32),
+            pltpu.VMEM((2, every, LANES), F32),
+            pltpu.VMEM((2, repeat, every), F32),
+            pltpu.VMEM((2, 2, block, ky), F32),
+            pltpu.SemaphoreType.DMA((2, 2)),
+        ],
         out_shape=jax.ShapeDtypeStruct((2, stokes, count, ky), F32),
+        compiler_params=pltpu.CompilerParams(vmem_limit_bytes=40 * 2**20),
         name="spectra",
-    )(first, mine, other, wiener)
+    )
+    held = pltpu.with_memory_space_constraint(held, pltpu.VMEM)
+    turns = pltpu.with_memory_space_constraint(turns, pltpu.VMEM)
+    return sum(
+        spectra(first, mine[at : at + parts], other[at : at + parts], held, turns)
+        for at in range(0, mine.shape[0], parts)
+    )
 
 
 def solution(mesh):

time: 68.9 us -> 55.2 us (0.80)
  Pallas kernels: 38.4 us -> 28.1 us
  waiting for transfers between devices: 13.4 us -> 6.57 us
  local copies, waits for them, and re-layouts: 3.34 us -> 8.06 us
  other arithmetic: 1.63 us -> 0.73 us
    pallas_call x1 -> x2, Pallas kernels: 27.5 us -> 17.2 us  [the longest x1 15.8 us: body(): spectra(first, mine[at:at + parts], other[at:at + parts], held, turns)]
    ppermute x3, waiting for transfers between devices: 9.65 us -> 2.85 us  [gather(): lax.ppermute(value, axis, [(i, (i + 2 * k) % size) for i in range(size)])]
    unnamed x8 -> x10, local copies, waits for them, and re-layouts: 1.47 us -> 6.18 us
    another operation x1, other arithmetic: 0.93 us -> 0.04 us  [gather(): mine = jnp.stack([own] + found)]
  transfers between devices with their start and end apart: 6 -> 6, of which waited for: 4 -> 3; matrix products, arithmetic and copies ran while one was open for 4% -> 5% of each run, Pallas kernels for 0% -> 2%
where the time goes in v2:
time: 55.2 us; the launch traced here: 54.9 us
  Pallas kernels  28.1 us (51%)
  starting transfers between devices  11.4 us (21%)
  local copies, waits for them, and re-layouts  8.06 us (15%)
  waiting for transfers between devices  6.57 us (12%)
  other arithmetic  0.73 us (1%)
    pallas_call x1, Pallas kernels, body(): spectra(first, mine[at:at + parts], other[at:at + parts], held, turns)  15.8 us
    pallas_call x1, Pallas kernels, body(): pl.pallas_call(functools.partial(bin_kernel, rows_own, col_blocks), out_s...  10.9 us
    ppermute x3, starting transfers between devices, gather(): lax.ppermute(value, axis, [(i, (i + 2 * k) % size) for i in range(size)])  7.63 us
    unnamed x10, local copies, waits for them, and re-layouts  6.18 us
    ppermute x3, waiting for transfers between devices, gather(): lax.ppermute(value, axis, [(i, (i + 2 * k) % size) for i in range(size)])  2.85 us
    ppermute x1, starting transfers between devices, neighbours(): lax.ppermute(value, axis, up)  2.4 us
    ppermute x1, waiting for transfers between devices, neighbours(): lax.ppermute(value, axis, [(j, i) for i, j in up])  1.94 us
    ppermute x1, waiting for transfers between devices, gather(): return (mine, lax.ppermute(mine, axis, [(i, i ^ 1) for i in range(size)]))  1.78 us
  transfers between devices with their start and end apart: 6, of which 3 were waited for; matrix products, arithmetic and copies ran while one was open for 5% of the time, Pallas kernels for 2%

profile of v2, /device:TPU:0, one launch (start us, length us, event | category | flops | bytes accessed | tf_op | source)
XLA Modules:
  0.0 54.9 jit_solution(18308849364711849141)
XLA Ops:
  0.0 2.4 %collective-permute-start = (bf16[512,256]{1,0:T(8,128)(2,1)}, bf16[512,256]{1,0:T(8,128)(2,1)S(1)}, u32[]{:S(2)}, u32[]{:S(2)}) collective-permute-start(bf16[512,256]{1,0:T(8,128)(2,1)} %own_ref.1), channel_id=1, source_target_pairs={{0,1},{1,2},{2,3},{3,4},{4,5},{5,6},{6,7},{8,9},{9,10},{10,11},{11... | collective-permute-start | bytes 786440 | tf_op jit(solution)/shard_map/ppermute | solution.py:272
  2.4 1.3 %collective-permute-start.1 = (bf16[512,256]{1,0:T(8,128)(2,1)}, bf16[512,256]{1,0:T(8,128)(2,1)S(1)}, u32[]{:S(2)}, u32[]{:S(2)}) collective-permute-start(bf16[512,256]{1,0:T(8,128)(2,1)} %own_ref.1), channel_id=1, source_target_pairs={{1,0},{2,1},{3,2},{4,3},{5,4},{6,5},{7,6},{9,8},{10,9},{11,10},{12... | collective-permute-start | bytes 786440 | tf_op jit(solution)/shard_map/ppermute | solution.py:272
  3.7 0.7 %pad_convert_fusion = f32[1152]{0:T(1024)S(1)} fusion(bf16[1025]{0:T(1024)(128)(2,1)} %param.14), kind=kLoop, calls=%fused_computation.1 | loop fusion | flops 1152 | bytes 6658 | tf_op jit(solution)/shard_map/reshape | solution.py:300
  4.4 0.6 %reshape.32.taps_ref = f32[1,1152]{1,0:T(1,128)} reshape(f32[1152]{0:T(1024)S(1)} %pad_convert_fusion) | data formatting | bytes 9216 | tf_op jit(solution)/shard_map/reshape | solution.py:300
  5.0 1.3 %pad.10.plate_ref = f32[8,128]{1,0:T(8,128)} pad(f32[4,128]{1,0:T(4,128)} %bitcast.14, f32[]{:T(128)} %constant.10.clone.1), padding=0_4x0_0 | pad | bytes 6148 | tf_op jit(solution)/shard_map/jit(_pad)/pad | solution.py:301
  6.3 0.0 collective-permute-done.before_ref
  6.3 0.0 copy-start.3
  6.3 1.9 %collective-permute-done.1.after_ref = bf16[512,256]{1,0:T(8,128)(2,1)S(1)} collective-permute-done((bf16[512,256]{1,0:T(8,128)(2,1)}, bf16[512,256]{1,0:T(8,128)(2,1)S(1)}, u32[]{:S(2)}, u32[]{:S(2)}) %collective-permute-start.1) | collective-permute-done | bytes 262176 | tf_op jit(solution)/shard_map/ppermute | solution.py:272
  8.2 0.0 copy-start.4
  8.2 0.0 copy-done.3
  8.2 0.7 %copy-done.4 = bf16[512,256]{1,0:T(8,128)(2,1)} copy-done((bf16[512,256]{1,0:T(8,128)(2,1)}, bf16[512,256]{1,0:T(8,128)(2,1)S(1)}, u32[]{:S(2)}) %copy-start.4) | copy-done | bytes 262168
  8.9 10.9 %bin_tiles.1.ready_ref = f32[72,384]{1,0:T(8,128)} custom-call(bf16[512,256]{1,0:T(8,128)(2,1)} %own_ref.1, bf16[512,256]{1,0:T(8,128)(2,1)} %copy-done.3, bf16[512,256]{1,0:T(8,128)(2,1)} %copy-done.4, f32[1,1152]{1,0:T(1,128)} %reshape.32.taps_ref, f32[8,128]{1,0:T(8,128)} %pad.10.plate_ref, f32[1,256]{1,0:T(1,128)} %bitcast.15, f32[1,256]{1,0:T(1,128)} %bitcast.16, ...), custom_call_target="tpu_custom_call" | custom-call | tf_op jit(solution)/shard_map/bin_tiles/pallas_call | solution.py:304
  19.8 6.6 %collective-permute-start.4 = (f32[72,384]{1,0:T(8,128)}, f32[72,384]{1,0:T(8,128)S(1)}, u32[]{:S(2)}, u32[]{:S(2)}) collective-permute-start(f32[72,384]{1,0:T(8,128)} %bin_tiles.1.ready_ref), channel_id=1, source_target_pairs={{0,6},{1,7},{2,0},{3,1},{4,2},{5,3},{6,4},{7,5},{8,14},{9,15},{10,... | collective-permute-start | bytes 331784 | tf_op jit(solution)/shard_map/ppermute | solution.py:281
  26.4 0.0 collective-permute-start.3
  26.5 1.0 %collective-permute-start.2 = (f32[72,384]{1,0:T(8,128)}, f32[72,384]{1,0:T(8,128)S(1)}, u32[]{:S(2)}, u32[]{:S(2)}) collective-permute-start(f32[72,384]{1,0:T(8,128)} %bin_tiles.1.ready_ref), channel_id=1, source_target_pairs={{0,2},{1,3},{2,4},{3,5},{4,6},{5,7},{6,0},{7,1},{8,10},{9,11},{10,... | collective-permute-start | bytes 331784 | tf_op jit(solution)/shard_map/ppermute | solution.py:281
  27.5 0.0 copy-start
  27.5 4.6 %copy-done = f32[3,512,2048]{2,1,0:T(8,128)S(1)} copy-done((f32[3,512,2048]{2,1,0:T(8,128)S(1)}, f32[3,512,2048]{2,1,0:T(8,128)}, u32[]{:S(2)}) %copy-start) | copy-done | bytes 12582936
  32.0 0.0 copy-start.1
  32.0 0.9 %copy-done.1 = f32[72,384]{1,0:T(8,128)S(1)} copy-done((f32[72,384]{1,0:T(8,128)S(1)}, f32[72,384]{1,0:T(8,128)}, u32[]{:S(2)}) %copy-start.1) | copy-done | bytes 110616
  32.9 0.0 copy-start.2
  32.9 1.3 %tables.1 = (f32[3,512,2048]{2,1,0:T(8,128)S(1)}, bf16[2,512,256]{2,1,0:T(8,128)(2,1)S(1)}) custom-call(s32[1]{0:T(128)} %bitcast.first_ref, f32[3,512,2048]{2,1,0:T(8,128)S(1)} %copy-done, f32[72,384]{1,0:T(8,128)S(1)} %copy-done.1), custom_call_target="tpu_custom_call" | custom-call | bytes 25165824 | tf_op jit(solution)/shard_map/tables/pallas_call | solution.py:324
  34.3 0.0 collective-permute-done.4
  34.3 2.8 %collective-permute-done.3 = f32[72,384]{1,0:T(8,128)S(1)} collective-permute-done((f32[72,384]{1,0:T(8,128)}, f32[72,384]{1,0:T(8,128)S(1)}, u32[]{:S(2)}, u32[]{:S(2)}) %collective-permute-start.3) | collective-permute-done | bytes 110624 | tf_op jit(solution)/shard_map/ppermute | solution.py:281
  37.1 0.0 collective-permute-done.2
  37.1 0.0 copy-done.2
  37.2 0.1 collective-permute-start.5
  37.2 1.8 %collective-permute-done.5.other_ref = f32[4,72,384]{2,1,0:T(8,128)S(1)} collective-permute-done((f32[4,72,384]{2,1,0:T(8,128)S(1)}, f32[4,72,384]{2,1,0:T(8,128)S(1)}, u32[]{:S(2)}, u32[]{:S(2)}) %collective-permute-start.5) | collective-permute-done | bytes 442400 | tf_op jit(solution)/shard_map/ppermute | solution.py:286
  39.0 15.8 %spectra.1 = f32[2,3,512,2048]{3,2,1,0:T(8,128)} custom-call(s32[1]{0:T(128)} %bitcast.first_ref, f32[4,72,384]{2,1,0:T(8,128)S(1)} %pad_maximum_fusion.mine_ref, f32[4,72,384]{2,1,0:T(8,128)S(1)} %collective-permute-done.5.other_ref, f32[3,512,2048]{2,1,0:T(8,128)S(1)} %get-tuple-element.10.wiener_ref, bf16[2,512,256]{2,1,0:T(8,128)(2,1)S(1)} %get-tuple-element.8.turns_ref), custom_call_target="tpu_custom_call" | custom-call | tf_op jit(solution)/shard_map/spectra/pallas_call | solution.py:360
  (1 shorter events, 0.0 us)
Async XLA Ops:
  0.0 6.3 %collective-permute-start = (bf16[512,256]{1,0:T(8,128)(2,1)}, bf16[512,256]{1,0:T(8,128)(2,1)S(1)}, u32[]{:S(2)}, u32[]{:S(2)}) collective-permute-start(bf16[512,256]{1,0:T(8,128)(2,1)} %own_ref.1), channel_id=1, source_target_pairs={{0,1},{1,2},{2,3},{3,4},{4,5},{5,6},{6,7},{8,9},{9,10},{10,11},{11... | collective-permute-start | bytes 786440 | tf_op jit(solution)/shard_map/ppermute | solution.py:272
  2.4 5.8 %collective-permute-start.1 = (bf16[512,256]{1,0:T(8,128)(2,1)}, bf16[512,256]{1,0:T(8,128)(2,1)S(1)}, u32[]{:S(2)}, u32[]{:S(2)}) collective-permute-start(bf16[512,256]{1,0:T(8,128)(2,1)} %own_ref.1), channel_id=1, source_target_pairs={{1,0},{2,1},{3,2},{4,3},{5,4},{6,5},{7,6},{9,8},{10,9},{11,10},{12... | collective-permute-start | bytes 786440 | tf_op jit(solution)/shard_map/ppermute | solution.py:272
  6.3 1.9 %copy-start.3 = (bf16[512,256]{1,0:T(8,128)(2,1)}, bf16[512,256]{1,0:T(8,128)(2,1)S(1)}, u32[]{:S(2)}) copy-start(bf16[512,256]{1,0:T(8,128)(2,1)S(1)} %collective-permute-done.before_ref) | copy-start | bytes 786436
  8.2 0.7 %copy-start.4 = (bf16[512,256]{1,0:T(8,128)(2,1)}, bf16[512,256]{1,0:T(8,128)(2,1)S(1)}, u32[]{:S(2)}) copy-start(bf16[512,256]{1,0:T(8,128)(2,1)S(1)} %collective-permute-done.1.after_ref) | copy-start | bytes 786436
  19.8 14.4 %collective-permute-start.4 = (f32[72,384]{1,0:T(8,128)}, f32[72,384]{1,0:T(8,128)S(1)}, u32[]{:S(2)}, u32[]{:S(2)}) collective-permute-start(f32[72,384]{1,0:T(8,128)} %bin_tiles.1.ready_ref), channel_id=1, source_target_pairs={{0,6},{1,7},{2,0},{3,1},{4,2},{5,3},{6,4},{7,5},{8,14},{9,15},{10,... | collective-permute-start | bytes 331784 | tf_op jit(solution)/shard_map/ppermute | solution.py:281
  26.4 10.7 %collective-permute-start.3 = (f32[72,384]{1,0:T(8,128)}, f32[72,384]{1,0:T(8,128)S(1)}, u32[]{:S(2)}, u32[]{:S(2)}) collective-permute-start(f32[72,384]{1,0:T(8,128)} %bin_tiles.1.ready_ref), channel_id=1, source_target_pairs={{0,4},{1,5},{2,6},{3,7},{4,0},{5,1},{6,2},{7,3},{8,12},{9,13},{10,... | collective-permute-start | bytes 331784 | tf_op jit(solution)/shard_map/ppermute | solution.py:281
  26.5 10.7 %collective-permute-start.2 = (f32[72,384]{1,0:T(8,128)}, f32[72,384]{1,0:T(8,128)S(1)}, u32[]{:S(2)}, u32[]{:S(2)}) collective-permute-start(f32[72,384]{1,0:T(8,128)} %bin_tiles.1.ready_ref), channel_id=1, source_target_pairs={{0,2},{1,3},{2,4},{3,5},{4,6},{5,7},{6,0},{7,1},{8,10},{9,11},{10,... | collective-permute-start | bytes 331784 | tf_op jit(solution)/shard_map/ppermute | solution.py:281
  27.5 4.6 %copy-start = (f32[3,512,2048]{2,1,0:T(8,128)S(1)}, f32[3,512,2048]{2,1,0:T(8,128)}, u32[]{:S(2)}) copy-start(f32[3,512,2048]{2,1,0:T(8,128)} %wiener_ref.1) | copy-start | bytes 37748740
  32.0 0.9 %copy-start.1 = (f32[72,384]{1,0:T(8,128)S(1)}, f32[72,384]{1,0:T(8,128)}, u32[]{:S(2)}) copy-start(f32[72,384]{1,0:T(8,128)} %bin_tiles.1.ready_ref) | copy-start | bytes 331780
  32.9 4.2 %copy-start.2 = (f32[72,384]{1,0:T(8,128)S(1)}, f32[72,384]{1,0:T(8,128)}, u32[]{:S(2)}) copy-start(f32[72,384]{1,0:T(8,128)} %bin_tiles.1.ready_ref) | copy-start | bytes 331780
  37.2 1.9 %collective-permute-start.5 = (f32[4,72,384]{2,1,0:T(8,128)S(1)}, f32[4,72,384]{2,1,0:T(8,128)S(1)}, u32[]{:S(2)}, u32[]{:S(2)}) collective-permute-start(f32[4,72,384]{2,1,0:T(8,128)S(1)} %pad_maximum_fusion.mine_ref), channel_id=1, source_target_pairs={{0,1},{1,0},{2,3},{3,2},{4,5},{5,4},{6,7},{7,6},{8,9},{9,8},{10,11... | collective-permute-start | bytes 1327112 | tf_op jit(solution)/shard_map/ppermute | solution.py:286

commit v3 on v2

v3 whole, which is shorter than its diff:
```python
import functools
import math

import jax
import jax.numpy as jnp
from jax import lax
from jax.experimental import pallas as pl
from jax.experimental.pallas import tpu as pltpu
from jax.sharding import PartitionSpec as P

PIECE = 16
LANES = 128
LOW = 16
HIGH = LANES // LOW
ROWS = 2048
COLS = 4096
SCALE = 1.0 / math.sqrt(ROWS * COLS)
GROUP = 16
F32 = jnp.float32
BF16 = jnp.bfloat16
NT = (((1,), (1,)), ((), ()))


def iota(shape, dim):
    return lax.broadcasted_iota(jnp.int32, shape, dim)


def turn(m, modulus):
    quarter = modulus // 4
    quadrant = (m + quarter // 2) // quarter if quarter & (quarter - 1) else (
        lax.shift_right_logical(m + quarter // 2, int(math.log2(quarter))))
    x = (m - quadrant * quarter).astype(F32) * (2.0 * math.pi / modulus)
    y = x * x
    s = x + x * y * (-1.0 / 6 + y * (1.0 / 120 + y * (-1.0 / 5040 + y * (1.0 / 362880))))
    c = 1.0 + y * (-0.5 + y * (1.0 / 24 + y * (-1.0 / 720 + y * (1.0 / 40320))))
    swap = (quadrant & 1) == 1
    cos = jnp.where(swap, s, c)
    sin = jnp.where(swap, c, s)
    cos = jnp.where(((quadrant + 1) & 2) == 2, -cos, cos)
    sin = jnp.where((quadrant & 2) == 2, -sin, sin)
    return cos, sin


def halves(value):
    high = value.astype(BF16)
    return high, (value - high.astype(F32)).astype(BF16)


def column(row):
    return jnp.transpose(jnp.broadcast_to(row, (LANES, LANES)))


def prepare_kernel(
    rows_own, col_blocks, tiles,
    pixel_ref, time_ref, small_ref,
    band_ref, factor_ref, high_ref, right_ref, own_ref, index_ref,
    low_ref,
):
    samples, dets = pixel_ref.shape
    groups = dets // LANES
    pieces = GROUP // groups
    width = band_ref.shape[1]
    own_ref[...] = time_ref[...]
    lines = [width // LANES, samples // LANES, groups, groups]
    starts = [sum(lines[:k]) for k in range(5)]

    def row(k):
        return jnp.concatenate(
            [small_ref[i : i + 1] for i in range(starts[k], starts[k] + lines[k])], axis=1
        )

    band_ref[...] = pltpu.roll(
        jnp.broadcast_to(row(0), (LANES, width)), 0, axis=1, stride=1, stride_axis=0
    ).astype(BF16)
    angle, weight = row(2), row(3)
    cos_det, sin_det = jnp.cos(2.0 * angle) * weight, jnp.sin(2.0 * angle) * weight
    quad = 4.0 * small_ref[starts[1] : starts[1] + lines[1]]
    cos_plate, sin_plate = jnp.cos(quad), jnp.sin(quad)
    for part in range(samples // LANES):
        span = slice(part * LANES, (part + 1) * LANES)
        cos_p = jnp.concatenate([column(cos_plate[part : part + 1])] * groups, axis=1)
        sin_p = jnp.concatenate([column(sin_plate[part : part + 1])] * groups, axis=1)
        factor_ref[0, span] = jnp.broadcast_to(weight, (LANES, dets))
        factor_ref[1, span] = cos_p * cos_det - sin_p * sin_det
        factor_ref[2, span] = sin_p * cos_det + cos_p * sin_det
    last = small_ref[starts[4] : starts[4] + 1]
    owner, block = last[:, :tiles].astype(jnp.int32), last[:, tiles : 2 * tiles].astype(jnp.int32)
    shift = int(math.log2(col_blocks))
    map_row = owner * rows_own + lax.shift_right_logical(block, shift)
    map_col = block & (col_blocks - 1)
    index_ref[...] = jnp.zeros_like(index_ref)
    for k, index in ((0, map_row), (1, map_col)):
        index_ref[k : k + 1, : 2 * tiles] = jnp.concatenate([index, index], axis=1).astype(F32)
    pixels = pixel_ref[...]
    high_ref[...] = lax.shift_right_logical(pixels, int(math.log2(LOW)))
    low_ref[...] = pixels & (LOW - 1)
    low_ids = iota((LOW, dets), 0)

    def piece_step(q, carry):
        g, p = lax.div(q, pieces), lax.rem(q, pieces)
        for t in range(PIECE):
            lanes = slice(t * LANES, (t + 1) * LANES)
            row = pl.ds(q * PIECE + t, 1)
            low = jnp.where(
                jnp.broadcast_to(low_ref[row, :], (LOW, dets)) == low_ids, 1.0, 0.0
            ).astype(BF16)
            for k in range(groups):
                at = pl.multiple_of((p * groups + k) * LOW, LOW)
                right_ref[g, pl.ds(at, LOW), lanes] = low[:, k * LANES : (k + 1) * LANES]
        return carry

    lax.fori_loop(0, samples // PIECE, piece_step, 0)


def bin_kernel(
    reach,
    place_ref, partner_ref, outside_ref, band_ref, factor_ref, high_ref, right_ref, own_ref, index_ref,
    out_ref,
    window, stokes, left,
):
    samples, dets = own_ref.shape
    groups = dets // LANES
    is_first = lax.rem(place_ref[0], 2) == 0
    window[reach : reach + samples] = own_ref[...]

    @pl.when(is_first)
    def _():
        window[:reach] = outside_ref[samples - reach :]
        window[reach + samples :] = partner_ref[:reach]

    @pl.when(jnp.logical_not(is_first))
    def _():
        window[:reach] = partner_ref[samples - reach :]
        window[reach + samples :] = outside_ref[:reach]

    width = band_ref.shape[1]
    for part in range(samples // LANES):
        span = slice(part * LANES, (part + 1) * LANES)
        filtered = jnp.dot(
            band_ref[...], window[part * LANES : part * LANES + width, :], preferred_element_type=F32
        )
        for s in range(3):
            stokes[s, span] = (filtered * factor_ref[s, span]).astype(BF16).astype(F32)
    high_ids = iota((HIGH, dets), 0)
    pieces = GROUP // groups
    mine = lax.div(iota((HIGH, LANES), 1), LOW) == iota((HIGH, LANES), 0)
    stack = GROUP * HIGH

    def group_step(g, carry):
        def piece_step(p, inner):
            first = (g * pieces + p) * PIECE
            for t in range(PIECE):
                row = pl.ds(first + t, 1)
                lanes = slice(t * LANES, (t + 1) * LANES)
                hot = jnp.broadcast_to(high_ref[row, :], (HIGH, dets)) == high_ids
                for s in range(3):
                    spread = jnp.where(hot, jnp.broadcast_to(stokes[s, row, :], (HIGH, dets)), 0.0)
                    both = jnp.concatenate(
                        [spread[:, k * LANES : (k + 1) * LANES] for k in range(groups)], axis=0
                    )
                    at = pl.multiple_of(s * stack + p * (groups * HIGH), groups * HIGH)
                    left[pl.ds(at, groups * HIGH), lanes] = both.astype(BF16)
            return inner

        lax.fori_loop(0, pieces, piece_step, 0)
        sums = lax.dot_general(left[...], right_ref[g], NT, preferred_element_type=F32)
        for s in range(3):
            rows = []
            for i in range(GROUP):
                start = (i * LOW) // LANES * LANES
                part = sums[s * stack + i * HIGH : s * stack + (i + 1) * HIGH, start : start + LANES]
                if start != i * LOW:
                    part = pltpu.roll(part, (start - i * LOW) % LANES, axis=1)
                part = pltpu.roll(part, 0, axis=1, stride=LOW, stride_axis=0)
                rows.append(jnp.sum(jnp.where(mine, part, 0.0), axis=0, keepdims=True))
            out_ref[pl.ds(pl.multiple_of(g * GROUP, GROUP), GROUP), s * LANES : (s + 1) * LANES] = (
                jnp.concatenate(rows, axis=0)
            )
        return carry

    tiles = out_ref.shape[0] - index_ref.shape[0]
    lax.fori_loop(0, tiles // GROUP, group_step, 0)
    out_ref[tiles:] = index_ref[...]


def table_kernel(place_ref, wiener_ref, ready_ref, held_ref, turns_ref, sem):
    del ready_ref
    copy = pltpu.make_async_copy(wiener_ref, held_ref, sem)
    copy.start()
    count = turns_ref.shape[1]
    first = place_ref[0] * count
    for at in range(0, count, LANES):
        size = min(LANES, count - at)
        kx = first + at + iota((size, LANES), 0)
        c, s = turn((kx * iota((size, LANES), 1)) & (COLS - 1), COLS)
        for k, value in enumerate((c * SCALE, s * -SCALE)):
            high, low = halves(value)
            turns_ref[k, at : at + size, :LANES] = high
            turns_ref[k, at : at + size, LANES:] = low
    copy.wait()


def expand(first, stack_ref, tiles, phases, table, start):
    parts = stack_ref.shape[0] // 2
    held = LANES // 2
    repeat = phases.shape[1]
    ky = table.shape[1]
    left_side = iota((1, LANES), 1) < held
    half_turns = 2 * ROWS - 1

    def build(p, carry):
        rows = pl.ds(pl.multiple_of(p * LANES, LANES), LANES)
        low, high = stack_ref.at[2 * p], stack_ref.at[2 * p + 1]
        tiles[pl.ds(pl.multiple_of(p * LANES, LANES), held)] = low[:held]
        tiles[pl.ds(pl.multiple_of(p * LANES + held, held), held)] = high[:held]
        r = jnp.where(left_side, low[held : held + 1, :LANES], high[held : held + 1, :LANES])
        b = jnp.where(left_side, low[held + 1 : held + 2, :LANES], high[held + 1 : held + 2, :LANES])
        kx = first + iota((repeat, LANES), 0)
        c, s = turn((r.astype(jnp.int32) - kx * b.astype(jnp.int32) * LANES) & half_turns, 2 * ROWS)
        phases[0, :, rows] = c
        phases[1, :, rows] = s
        down = column(r).astype(jnp.int32)
        c, s = turn((r.astype(jnp.int32) * (2 * LANES)) & half_turns, 2 * ROWS)
        turn_c, turn_s = column(c), column(s)
        for g in range(0, LANES, 16):
            some = slice(g, g + 16)
            c, s = turn((down[some] * (2 * iota((16, LANES), 1) + 1)) & half_turns, 2 * ROWS)
            cs, ss = turn_c[some], turn_s[some]
            at = pl.ds(pl.multiple_of(start + p * LANES + g, 16), 16)
            for n in range(0, ky, 2 * LANES):
                table[at, n : n + LANES] = c.astype(BF16)
                table[at, n + LANES : n + 2 * LANES] = s.astype(BF16)
                c, s = c * cs - s * ss, c * ss + s * cs
        return carry

    lax.fori_loop(0, parts, build, 0, unroll=parts <= 4)


def factors(tiles, phases, turns_ref, rows, channel, at, size):
    high, low = halves(tiles[rows, channel])
    twice = jnp.concatenate([high, high], axis=1)
    real, imag = [
        lax.dot_general(turns_ref[side, at], twice, NT, preferred_element_type=F32)
        + lax.dot_general(turns_ref[side, at, :LANES], low, NT, preferred_element_type=F32)
        for side in range(2)
    ]
    pc = jnp.concatenate([phases[0, :, rows]] * (size // phases.shape[1]), axis=0)
    ps = jnp.concatenate([phases[1, :, rows]] * (size // phases.shape[1]), axis=0)
    return (real * pc - imag * ps).astype(BF16), (real * ps + imag * pc).astype(BF16)


def early_kernel(block, place_ref, stack_ref, turns_ref, factor_ref, table_ref, tiles, phases):
    stokes, count = factor_ref.shape[0], factor_ref.shape[1] // 2
    expand(place_ref[0] * count, stack_ref, tiles, phases, table_ref, 0)
    for s in range(stokes):
        channel = slice(s * LANES, (s + 1) * LANES)
        for k in range(0, count, block):
            real, imag = factors(
                tiles, phases, turns_ref, slice(None), channel, slice(k, k + block), block
            )
            factor_ref[s, k : k + block] = real
            factor_ref[s, count + k : count + k + block] = imag


def spectrum_kernel(early, place_ref, stack_ref, wiener_ref, turns_ref, *refs):
    ready_factor, ready_table = refs[:2] if early else (None, None)
    out_ref, tiles, factor, table, phases, buffer, sems = refs[2 * early :]
    stokes, count, ky = wiener_ref.shape
    block = factor.shape[0] // 2
    own = tiles.shape[0]
    ready = table.shape[0] - own
    if early:
        table[:ready] = ready_table[...]
    expand(place_ref[0] * count, stack_ref, tiles, phases, table, ready)
    half = ky // 2
    width = min(4 * LANES, own)
    flip = LANES - 1 - iota((block, LANES), 1)

    quarter = half // 2
    spans = ((0, quarter), (ky - quarter, quarter), (quarter, half))

    def copies(i, slot, which):
        s, k = lax.div(i, count // block), lax.rem(i, count // block)
        at = pl.ds(pl.multiple_of(k * block, block), block)
        for j in which:
            lanes = pl.ds(*spans[j])
            for side in range(2):
                yield pltpu.make_async_copy(
                    buffer.at[slot, side, :, lanes], out_ref.at[side, s, at, lanes], sems.at[slot, side, j]
                )

    def step(i, carry):
        slot = lax.rem(i, 2)
        s, k = lax.div(i, count // block), lax.rem(i, count // block)
        at = pl.ds(pl.multiple_of(k * block, block), block)
        channel = pl.ds(pl.multiple_of(s * LANES, LANES), LANES)

        def make(q, inner):
            rows = pl.ds(pl.multiple_of(q * width, width), width)
            into = pl.ds(pl.multiple_of(ready + q * width, LANES), width)
            real, imag = factors(tiles, phases, turns_ref, rows, channel, at, block)
            factor[:block, into] = real
            factor[block:, into] = imag
            return inner

        lax.fori_loop(0, own // width, make, 0)
        if early:
            under = pl.ds(pl.multiple_of(count + k * block, block), block)
            factor[:block, :ready] = ready_factor[s, at]
            factor[block:, :ready] = ready_factor[s, under]

        @pl.when(i >= 2)
        def _():
            for copy in copies(i, slot, (0, 1, 2)):
                copy.wait()

        for n in range(half // LANES):
            lanes = slice(n * LANES, (n + 1) * LANES)
            back = slice(ky - (n + 1) * LANES, ky - n * LANES)
            both = jnp.dot(
                factor[...], table[:, 2 * n * LANES : 2 * (n + 1) * LANES], preferred_element_type=F32
            )
            re_even, re_odd = both[:block, :LANES], both[:block, LANES:]
            im_even, im_odd = both[block:, :LANES], both[block:, LANES:]
            weight = wiener_ref[s, at, lanes]
            buffer[slot, 0, :, lanes] = (re_even + im_odd) * weight
            buffer[slot, 1, :, lanes] = (im_even - re_odd) * weight
            weight = wiener_ref[s, at, back]
            buffer[slot, 0, :, back] = jnp.take_along_axis(re_even - im_odd, flip, axis=1) * weight
            buffer[slot, 1, :, back] = jnp.take_along_axis(im_even + re_odd, flip, axis=1) * weight
            if (n + 1) * LANES == quarter:
                for copy in copies(i, slot, (0, 1)):
                    copy.start()
        for copy in copies(i, slot, (2,)):
            copy.start()
        return carry

    steps = stokes * (count // block)
    lax.fori_loop(0, steps, step, 0)
    for i in (steps - 2, steps - 1):
        for copy in copies(i, i % 2, (0, 1, 2)):
            copy.wait()


def neighbours(value, axis):
    size = lax.axis_size(axis)
    outer = [(i, i + 1) for i in range(1, size - 1, 2)]
    outside = lax.ppermute(value, axis, outer + [(j, i) for i, j in outer])
    return lax.ppermute(value, axis, [(i, i ^ 1) for i in range(size)]), outside


def gather(value, ready, axis):
    size = lax.axis_size(axis)
    most = 32
    if size > 8:
        whole = lax.all_gather(value, axis, axis=0)
        return [whole[at : at + most] for at in range(0, size, most)]
    found = [
        lax.ppermute(value, axis, [(i, i ^ (2 * k)) for i in range(size)]) for k in range(1, size // 2)
    ]
    own, _ = lax.optimization_barrier((value, ready))
    mine = jnp.stack([own] + found)
    return [mine, lax.ppermute(mine, axis, [(i, i ^ 1) for i in range(size)])]


def body(
    timeline, pointing, plate_angle, detector_angle, detector_weight, kernel, tile_owner, tile_block, wiener
):
    samples, dets = timeline.shape
    tiles = tile_owner.shape[0]
    devices = lax.axis_size("tm")
    partner, outside = neighbours(timeline, "tm")
    count_taps = kernel.shape[0]
    reach = (count_taps - 1) // 2
    width = count_taps - 1 + LANES
    pieces = [
        jnp.pad(kernel.astype(F32), (0, width - count_taps)), plate_angle, detector_angle, detector_weight,
        tile_owner.reshape(tiles).astype(F32), tile_block.reshape(tiles).astype(F32),
    ]
    used = sum(piece.shape[0] for piece in pieces)
    small = jnp.pad(jnp.concatenate(pieces), (0, -used % (8 * LANES))).reshape(-1, LANES)
    rows_own = ROWS // devices
    col_blocks = COLS // LANES
    vmem, hbm = pl.BlockSpec(memory_space=pltpu.VMEM), pl.BlockSpec(memory_space=pltpu.HBM)
    scalar = pl.BlockSpec(memory_space=pltpu.SMEM)
    place = lax.axis_index("tm").astype(jnp.int32).reshape(1)
    prepared = pl.pallas_call(
        functools.partial(prepare_kernel, rows_own, col_blocks, tiles),
        out_specs=[vmem] * 6,
        out_shape=[
            pltpu.VMEM((LANES, width), BF16),
            pltpu.VMEM((3, samples, dets), F32),
            pltpu.VMEM((samples, dets), jnp.int32),
            pltpu.VMEM((tiles // GROUP, GROUP * LOW, PIECE * LANES), BF16),
            pltpu.VMEM((samples, dets), BF16),
            pltpu.VMEM((8, 3 * LANES), F32),
        ],
        scratch_shapes=[pltpu.VMEM((samples, dets), jnp.int32)],
        compiler_params=pltpu.CompilerParams(vmem_limit_bytes=32 * 2**20),
        cost_estimate=pl.CostEstimate(flops=0, bytes_accessed=2**23, transcendentals=0),
        name="prepare",
    )(pointing, timeline, small)
    packed = pl.pallas_call(
        functools.partial(bin_kernel, reach),
        in_specs=[scalar] + [vmem] * 8,
        out_shape=jax.ShapeDtypeStruct((tiles + 8, 3 * LANES), F32),
        scratch_shapes=[
            pltpu.VMEM((2 * reach + samples, dets), BF16),
            pltpu.VMEM((3, samples, dets), F32),
            pltpu.VMEM((3 * GROUP * HIGH, PIECE * LANES), BF16),
        ],
        compiler_params=pltpu.CompilerParams(vmem_limit_bytes=40 * 2**20),
        name="bin_tiles",
    )(place, partner, outside, *[pltpu.with_memory_space_constraint(v, pltpu.VMEM) for v in prepared])
    stokes, count, ky = wiener.shape
    held, turns = pl.pallas_call(
        table_kernel,
        in_specs=[scalar, hbm, pl.BlockSpec(memory_space=pl.ANY)],
        out_specs=[vmem, vmem],
        out_shape=[pltpu.VMEM(wiener.shape, F32), pltpu.VMEM((2, count, 2 * LANES), BF16)],
        scratch_shapes=[pltpu.SemaphoreType.DMA],
        compiler_params=pltpu.CompilerParams(vmem_limit_bytes=4 * 2**20),
        cost_estimate=pl.CostEstimate(flops=0, bytes_accessed=2 * wiener.size * 4, transcendentals=0),
        name="tables",
    )(place, wiener, packed)
    in_vmem = functools.partial(pltpu.with_memory_space_constraint, memory_space=pltpu.VMEM)
    stacks = gather(packed, turns, "tm")
    held, turns = in_vmem(held), in_vmem(turns)
    early = len(stacks) == 2
    block = min(256, count)
    repeat = min(COLS // LANES, block)
    every = stacks[0].shape[0] // 2 * LANES
    lists = [pltpu.VMEM((every, 3 * LANES), F32), pltpu.VMEM((2, repeat, every), F32)]
    more = []
    if early:
        more = pl.pallas_call(
            functools.partial(early_kernel, block),
            in_specs=[scalar, vmem, vmem],
            out_specs=[vmem, vmem],
            scratch_shapes=lists,
            out_shape=[pltpu.VMEM((stokes, 2 * count, every), BF16), pltpu.VMEM((every, ky), BF16)],
            compiler_params=pltpu.CompilerParams(vmem_limit_bytes=12 * 2**20),
            cost_estimate=pl.CostEstimate(
                flops=12 * stokes * count * every * LANES, bytes_accessed=2**22, transcendentals=0
            ),
            name="early_factors",
        )(place, stacks.pop(0), turns)
        more = [in_vmem(v) for v in more]
    columns = every * (1 + early)
    spectra = pl.pallas_call(
        functools.partial(spectrum_kernel, early),
        in_specs=[scalar] + [vmem] * (3 + len(more)),
        out_specs=hbm,
        scratch_shapes=[
            lists[0],
            pltpu.VMEM((2 * block, columns), BF16),
            pltpu.VMEM((columns, ky), BF16),
            lists[1],
            pltpu.VMEM((2, 2, block, ky), F32),
            pltpu.SemaphoreType.DMA((2, 2, 3)),
        ],
        out_shape=jax.ShapeDtypeStruct((2, stokes, count, ky), F32),
        compiler_params=pltpu.CompilerParams(vmem_limit_bytes=40 * 2**20),
        name="spectra",
    )
    return sum(spectra(place, stack, held, turns, *more) for stack in stacks)


def solution(mesh):
    placed = (
        P("tm", "band"), P("tm", "band"), P("tm"), P("band"), P("band"), P("band"),
        P("tm", "band"), P("tm", "band"), P("band", "tm", None),
    )
    return jax.shard_map(
        body, mesh=mesh, in_specs=placed, out_specs=P(None, "band", "tm", None), check_vma=False
    )
```

time: 55.2 us -> 45.4 us (0.82)
  Pallas kernels: 28.1 us -> 23.8 us
  waiting for transfers between devices: 6.57 us -> 3 us
  starting transfers between devices: 11.4 us -> 8.72 us
  other arithmetic: 0.73 us -> 1.4 us
    pallas_call x2 -> x4, Pallas kernels: 26.7 us -> 22.4 us  [the longest x1 13.5 us: body(): return sum((spectra(place, stack, held, turns, *more) for stack in stacks))]
    ppermute x6, waiting for transfers between devices: 6.57 us -> 3 us  [the longest x3 2.88 us: gather(): lax.ppermute(value, axis, [(i, i ^ 2 * k) for i in range(size)])]
    ppermute x6, starting transfers between devices: 11.4 us -> 8.72 us  [the longest x3 7.08 us: gather(): lax.ppermute(value, axis, [(i, i ^ 2 * k) for i in range(size)])]
    pad x1 -> x0, local copies, waits for them, and re-layouts: 1.28 us -> none  [body(): jnp.pad(plate_angle.reshape(samples // LANES, LANES), ((0, 8 - samples //...]
    unnamed x10 -> x8, local copies, waits for them, and re-layouts: 6.18 us -> 7.34 us
    concatenate x0 -> x1, local copies, waits for them, and re-layouts: none -> 0.78 us  [body(): jnp.concatenate(pieces)]
    reshape x1 -> x0, other arithmetic: 0.69 us -> none  [body(): jnp.pad(kernel.astype(F32), (0, width - count_taps)).reshape(1, width)]
    pad x0 -> x1, other arithmetic: none -> 0.69 us  [body(): jnp.pad(kernel.astype(F32), (0, width - count_taps))]
  transfers between devices with their start and end apart: 6 -> 6, of which waited for: 3 -> 2; matrix products, arithmetic and copies ran while one was open for 5% -> 5% of each run, Pallas kernels for 2% -> 10%
where the time goes in v3:
time: 45.4 us; the launch traced here: 45.1 us
  Pallas kernels  23.8 us (52%)
  starting transfers between devices  8.72 us (19%)
  local copies, waits for them, and re-layouts  8.13 us (18%)
  waiting for transfers between devices  3 us (7%)
  other arithmetic  1.4 us (3%)
    pallas_call x1, Pallas kernels, body(): return sum((spectra(place, stack, held, turns, *more) for stack in stacks))  13.5 us
    unnamed x8, local copies, waits for them, and re-layouts  7.34 us
    ppermute x3, starting transfers between devices, gather(): lax.ppermute(value, axis, [(i, i ^ 2 * k) for i in range(size)])  7.08 us
    pallas_call x1, Pallas kernels, body(): pl.pallas_call(functools.partial(bin_kernel, reach), in_specs=[scalar] +...  5.78 us
    ppermute x3, waiting for transfers between devices, gather(): lax.ppermute(value, axis, [(i, i ^ 2 * k) for i in range(size)])  2.88 us
    pallas_call x1, Pallas kernels, body(): pl.pallas_call(functools.partial(prepare_kernel, rows_own, col_blocks, ti...  1.9 us
    pallas_call x1, Pallas kernels, body(): pl.pallas_call(table_kernel, in_specs=[scalar, hbm, pl.BlockSpec(memory_s...  1.31 us
    pallas_call x1, Pallas kernels, body(): pl.pallas_call(functools.partial(early_kernel, block), in_specs=[scalar,...  1.3 us
  transfers between devices with their start and end apart: 6, of which 2 were waited for; matrix products, arithmetic and copies ran while one was open for 5% of the time, Pallas kernels for 10%

profile of v3, /device:TPU:0, one launch (start us, length us, event | category | flops | bytes accessed | tf_op | source)
XLA Modules:
  0.0 45.1 jit_solution(866393317168715161)
XLA Ops:
  0.0 0.5 %collective-permute-start = (bf16[512,256]{1,0:T(8,128)(2,1)}, bf16[512,256]{1,0:T(8,128)(2,1)S(1)}, u32[]{:S(2)}, u32[]{:S(2)}) collective-permute-start(bf16[512,256]{1,0:T(8,128)(2,1)} %time_ref.1), channel_id=1, source_target_pairs={{0,1},{1,0},{2,3},{3,2},{4,5},{5,4},{6,7},{7,6},{8,9},{9,8},{10,11... | collective-permute-start | bytes 786440 | tf_op jit(solution)/shard_map/ppermute | solution.py:349
  0.5 0.7 %collective-permute-start.1 = (bf16[512,256]{1,0:T(8,128)(2,1)}, bf16[512,256]{1,0:T(8,128)(2,1)S(1)}, u32[]{:S(2)}, u32[]{:S(2)}) collective-permute-start(bf16[512,256]{1,0:T(8,128)(2,1)} %time_ref.1), channel_id=1, source_target_pairs={{1,2},{3,4},{5,6},{2,1},{4,3},{6,5},{9,10},{11,12},{13,14},{10,9},... | collective-permute-start | bytes 786440 | tf_op jit(solution)/shard_map/ppermute | solution.py:348
  1.2 0.7 %convert_bitcast_fusion = (f32[64]{0:T(128)S(1)}, f32[64]{0:T(128)S(1)}) fusion(s32[64,1]{0,1:T(1,128)} %param.16, s32[64,1]{0,1:T(1,128)} %param.15), kind=kLoop, calls=%fused_computation.3 | loop fusion | flops 128 | bytes 1024 | tf_op jit(solution)/shard_map/convert_element_type | solution.py:378
  1.8 0.7 %pad_convert_fusion = f32[1152]{0:T(1024)S(1)} fusion(bf16[1025]{0:T(1024)(128)(2,1)} %param.14), kind=kLoop, calls=%fused_computation.2 | loop fusion | flops 1152 | bytes 6658 | tf_op jit(solution)/shard_map/jit(_pad)/pad | solution.py:377
  2.5 0.8 %concatenate.3 = f32[2304]{0:T(1024)S(1)} concatenate(f32[1152]{0:T(1024)S(1)} %pad_convert_fusion, f32[512]{0:T(512)} %param.11, f32[256]{0:T(256)} %param.12, f32[256]{0:T(256)} %param.13, f32[64]{0:T(128)S(1)} %get-tuple-element.28, f32[64]{0:T(128)S(1)} %get-tuple-element.27), dimensions={0} | concatenate | bytes 18432 | tf_op jit(solution)/shard_map/concatenate | solution.py:381
  3.3 0.0 copy-start.1
  3.3 1.0 %copy-done.1 = s32[512,256]{1,0:T(8,128)S(1)} copy-done((s32[512,256]{1,0:T(8,128)S(1)}, s32[512,256]{1,0:T(8,128)}, u32[]{:S(2)}) %copy-start.1) | copy-done | bytes 524312
  4.4 0.0 copy-start.2
  4.4 0.9 %copy-done.2 = bf16[512,256]{1,0:T(8,128)(2,1)S(1)} copy-done((bf16[512,256]{1,0:T(8,128)(2,1)S(1)}, bf16[512,256]{1,0:T(8,128)(2,1)}, u32[]{:S(2)}) %copy-start.2) | copy-done | bytes 262168
  5.3 1.9 %prepare.1 = (bf16[128,1152]{1,0:T(8,128)(2,1)S(1)}, f32[3,512,256]{2,1,0:T(8,128)S(1)}, s32[512,256]{1,0:T(8,128)S(1)}, bf16[4,256,2048]{2,1,0:T(8,128)(2,1)S(1...) custom-call(s32[512,256]{1,0:T(8,128)S(1)} %copy-done.1, bf16[512,256]{1,0:T(8,128)(2,1)S(1)} %copy-done.2, ...), custom_call_target="tpu_custom_call" | custom-call | bytes 8388608 | tf_op jit(solution)/shard_map/prepare/pallas_call | solution.py:387
  7.2 0.0 collective-permute-done.partner_ref
  7.2 0.0 collective-permute-done.1.outside_ref
  7.2 5.8 %bin_tiles.1.ready_ref = f32[72,384]{1,0:T(8,128)S(1)} custom-call(s32[1]{0:T(128)} %bitcast.place_ref, bf16[512,256]{1,0:T(8,128)(2,1)S(1)} %collective-permute-done.partner_ref, bf16[512,256]{1,0:T(8,128)(2,1)S(1)} %collective-permute-done.1.outside_ref, bf16[128,1152]{1,0:T(8,128)(2,1)S(1)} %get-tuple-element.16.band_ref, ...), custom_call_target="tpu_custom_call" | custom-call | tf_op jit(solution)/shard_map/bin_tiles/pallas_call | solution.py:403
  13.0 6.4 %collective-permute-start.4 = (f32[72,384]{1,0:T(8,128)S(1)}, f32[72,384]{1,0:T(8,128)S(1)}, u32[]{:S(2)}, u32[]{:S(2)}) collective-permute-start(f32[72,384]{1,0:T(8,128)S(1)} %bin_tiles.1.ready_ref), channel_id=1, source_target_pairs={{0,6},{1,7},{2,4},{3,5},{4,2},{5,3},{6,0},{7,1},{8,14},{9,15},{10,... | collective-permute-start | bytes 331784 | tf_op jit(solution)/shard_map/ppermute | solution.py:359
  19.5 0.0 collective-permute-start.3
  19.5 0.6 %collective-permute-start.2 = (f32[72,384]{1,0:T(8,128)S(1)}, f32[72,384]{1,0:T(8,128)S(1)}, u32[]{:S(2)}, u32[]{:S(2)}) collective-permute-start(f32[72,384]{1,0:T(8,128)S(1)} %bin_tiles.1.ready_ref), channel_id=1, source_target_pairs={{0,2},{1,3},{2,0},{3,1},{4,6},{5,7},{6,4},{7,5},{8,10},{9,11},{10,... | collective-permute-start | bytes 331784 | tf_op jit(solution)/shard_map/ppermute | solution.py:359
  20.1 0.0 copy-start
  20.1 4.6 %copy-done = f32[3,512,2048]{2,1,0:T(8,128)S(1)} copy-done((f32[3,512,2048]{2,1,0:T(8,128)S(1)}, f32[3,512,2048]{2,1,0:T(8,128)}, u32[]{:S(2)}) %copy-start) | copy-done | bytes 12582936
  24.7 1.3 %tables.1 = (f32[3,512,2048]{2,1,0:T(8,128)S(1)}, bf16[2,512,256]{2,1,0:T(8,128)(2,1)S(1)}) custom-call(s32[1]{0:T(128)} %bitcast.place_ref, f32[3,512,2048]{2,1,0:T(8,128)S(1)} %copy-done, f32[72,384]{1,0:T(8,128)S(1)} %bin_tiles.1.ready_ref), custom_call_target="tpu_custom_call" | custom-call | bytes 25165824 | tf_op jit(solution)/shard_map/tables/pallas_call | solution.py:416
  26.0 0.0 collective-permute-done.4
  26.0 2.9 %collective-permute-done.3 = f32[72,384]{1,0:T(8,128)S(1)} collective-permute-done((f32[72,384]{1,0:T(8,128)S(1)}, f32[72,384]{1,0:T(8,128)S(1)}, u32[]{:S(2)}, u32[]{:S(2)}) %collective-permute-start.3) | collective-permute-done | bytes 110624 | tf_op jit(solution)/shard_map/ppermute | solution.py:359
  28.9 0.0 collective-permute-done.2
  28.9 0.5 %collective-permute-start.5 = (f32[4,72,384]{2,1,0:T(8,128)S(1)}, f32[4,72,384]{2,1,0:T(8,128)S(1)}, u32[]{:S(2)}, u32[]{:S(2)}) collective-permute-start(f32[4,72,384]{2,1,0:T(8,128)S(1)} %pad_maximum_fusion.stack_ref), channel_id=1, source_target_pairs={{0,1},{1,0},{2,3},{3,2},{4,5},{5,4},{6,7},{7,6},{8,9},{9,8},{10,11... | collective-permute-start | bytes 1327112 | tf_op jit(solution)/shard_map/ppermute | solution.py:363
  29.4 1.3 %early_factors.1 = (bf16[3,1024,256]{2,1,0:T(8,128)(2,1)S(1)}, bf16[256,2048]{1,0:T(8,128)(2,1)S(1)}) custom-call(s32[1]{0:T(128)} %bitcast.place_ref, f32[4,72,384]{2,1,0:T(8,128)S(1)} %pad_maximum_fusion.stack_ref, bf16[2,512,256]{2,1,0:T(8,128)(2,1)S(1)} %get-tuple-element.22.turns_ref), custom_call_target="tpu_custom_call" | custom-call | flops 603979776 | bytes 4194304 | tf_op jit(solution)/shard_map/early_factors/pallas_call | solution.py:436
  30.7 0.1 collective-permute-done.5.stack_ref
  30.8 0.0 copy-start.3
  30.8 0.8 %copy-done.3 = f32[4,72,384]{2,1,0:T(8,128)} copy-done((f32[4,72,384]{2,1,0:T(8,128)}, f32[4,72,384]{2,1,0:T(8,128)S(1)}, u32[]{:S(2)}) %copy-start.3) | copy-done | bytes 442392
  31.6 13.5 %spectra.1 = f32[2,3,512,2048]{3,2,1,0:T(8,128)} custom-call(s32[1]{0:T(128)} %bitcast.place_ref, f32[4,72,384]{2,1,0:T(8,128)} %copy-done.3, f32[3,512,2048]{2,1,0:T(8,128)S(1)} %get-tuple-element.24.wiener_ref, bf16[2,512,256]{2,1,0:T(8,128)(2,1)S(1)} %get-tuple-element.22.turns_ref, bf16[3,1024,256]{2,1,0:T(8,128)(2,1)S(1)} %get-tuple-element.25.refs_0_, ...), custom_call_target="tpu_custom_call" | custom-call | tf_op jit(solution)/shard_map/spectra/pallas_call | solution.py:466
  (2 shorter events, 0.0 us)
Async XLA Ops:
  0.0 7.2 %collective-permute-start = (bf16[512,256]{1,0:T(8,128)(2,1)}, bf16[512,256]{1,0:T(8,128)(2,1)S(1)}, u32[]{:S(2)}, u32[]{:S(2)}) collective-permute-start(bf16[512,256]{1,0:T(8,128)(2,1)} %time_ref.1), channel_id=1, source_target_pairs={{0,1},{1,0},{2,3},{3,2},{4,5},{5,4},{6,7},{7,6},{8,9},{9,8},{10,11... | collective-permute-start | bytes 786440 | tf_op jit(solution)/shard_map/ppermute | solution.py:349
  0.5 6.7 %collective-permute-start.1 = (bf16[512,256]{1,0:T(8,128)(2,1)}, bf16[512,256]{1,0:T(8,128)(2,1)S(1)}, u32[]{:S(2)}, u32[]{:S(2)}) collective-permute-start(bf16[512,256]{1,0:T(8,128)(2,1)} %time_ref.1), channel_id=1, source_target_pairs={{1,2},{3,4},{5,6},{2,1},{4,3},{6,5},{9,10},{11,12},{13,14},{10,9},... | collective-permute-start | bytes 786440 | tf_op jit(solution)/shard_map/ppermute | solution.py:348
  3.3 1.0 %copy-start.1 = (s32[512,256]{1,0:T(8,128)S(1)}, s32[512,256]{1,0:T(8,128)}, u32[]{:S(2)}) copy-start(s32[512,256]{1,0:T(8,128)} %pixel_ref.1) | copy-start | bytes 1572868
  4.4 0.9 %copy-start.2 = (bf16[512,256]{1,0:T(8,128)(2,1)S(1)}, bf16[512,256]{1,0:T(8,128)(2,1)}, u32[]{:S(2)}) copy-start(bf16[512,256]{1,0:T(8,128)(2,1)} %time_ref.1) | copy-start | bytes 786436
  13.0 13.0 %collective-permute-start.4 = (f32[72,384]{1,0:T(8,128)S(1)}, f32[72,384]{1,0:T(8,128)S(1)}, u32[]{:S(2)}, u32[]{:S(2)}) collective-permute-start(f32[72,384]{1,0:T(8,128)S(1)} %bin_tiles.1.ready_ref), channel_id=1, source_target_pairs={{0,6},{1,7},{2,4},{3,5},{4,2},{5,3},{6,0},{7,1},{8,14},{9,15},{10,... | collective-permute-start | bytes 331784 | tf_op jit(solution)/shard_map/ppermute | solution.py:359
  19.5 9.4 %collective-permute-start.3 = (f32[72,384]{1,0:T(8,128)S(1)}, f32[72,384]{1,0:T(8,128)S(1)}, u32[]{:S(2)}, u32[]{:S(2)}) collective-permute-start(f32[72,384]{1,0:T(8,128)S(1)} %bin_tiles.1.ready_ref), channel_id=1, source_target_pairs={{0,4},{1,5},{2,6},{3,7},{4,0},{5,1},{6,2},{7,3},{8,12},{9,13},{10,... | collective-permute-start | bytes 331784 | tf_op jit(solution)/shard_map/ppermute | solution.py:359
  19.5 9.4 %collective-permute-start.2 = (f32[72,384]{1,0:T(8,128)S(1)}, f32[72,384]{1,0:T(8,128)S(1)}, u32[]{:S(2)}, u32[]{:S(2)}) collective-permute-start(f32[72,384]{1,0:T(8,128)S(1)} %bin_tiles.1.ready_ref), channel_id=1, source_target_pairs={{0,2},{1,3},{2,0},{3,1},{4,6},{5,7},{6,4},{7,5},{8,10},{9,11},{10,... | collective-permute-start | bytes 331784 | tf_op jit(solution)/shard_map/ppermute | solution.py:359
  20.1 4.6 %copy-start = (f32[3,512,2048]{2,1,0:T(8,128)S(1)}, f32[3,512,2048]{2,1,0:T(8,128)}, u32[]{:S(2)}) copy-start(f32[3,512,2048]{2,1,0:T(8,128)} %wiener_ref.1) | copy-start | bytes 37748740
  28.9 1.9 %collective-permute-start.5 = (f32[4,72,384]{2,1,0:T(8,128)S(1)}, f32[4,72,384]{2,1,0:T(8,128)S(1)}, u32[]{:S(2)}, u32[]{:S(2)}) collective-permute-start(f32[4,72,384]{2,1,0:T(8,128)S(1)} %pad_maximum_fusion.stack_ref), channel_id=1, source_target_pairs={{0,1},{1,0},{2,3},{3,2},{4,5},{5,4},{6,7},{7,6},{8,9},{9,8},{10,11... | collective-permute-start | bytes 1327112 | tf_op jit(solution)/shard_map/ppermute | solution.py:363
  30.8 0.8 %copy-start.3 = (f32[4,72,384]{2,1,0:T(8,128)}, f32[4,72,384]{2,1,0:T(8,128)S(1)}, u32[]{:S(2)}) copy-start(f32[4,72,384]{2,1,0:T(8,128)S(1)} %collective-permute-done.5.stack_ref) | copy-start | bytes 1327108

commit v4 on v3

--- a/solution.py
+++ b/solution.py
@@ -51,30 +51,25 @@
 
 
 def prepare_kernel(
-    rows_own, col_blocks, tiles,
-    pixel_ref, time_ref, small_ref,
+    rows_own, col_blocks,
+    pixel_ref, time_ref, kernel_ref, plate_ref, angle_ref, weight_ref, owner_ref, block_ref,
     band_ref, factor_ref, high_ref, right_ref, own_ref, index_ref,
-    low_ref,
+    low_ref, padded,
 ):
     samples, dets = pixel_ref.shape
     groups = dets // LANES
     pieces = GROUP // groups
     width = band_ref.shape[1]
     own_ref[...] = time_ref[...]
-    lines = [width // LANES, samples // LANES, groups, groups]
-    starts = [sum(lines[:k]) for k in range(5)]
-
-    def row(k):
-        return jnp.concatenate(
-            [small_ref[i : i + 1] for i in range(starts[k], starts[k] + lines[k])], axis=1
-        )
-
+    count = kernel_ref.shape[1]
+    padded[...] = jnp.zeros_like(padded)
+    padded[:, :count] = kernel_ref[...].astype(F32)
     band_ref[...] = pltpu.roll(
-        jnp.broadcast_to(row(0), (LANES, width)), 0, axis=1, stride=1, stride_axis=0
+        jnp.broadcast_to(padded[...], (LANES, width)), 0, axis=1, stride=1, stride_axis=0
     ).astype(BF16)
-    angle, weight = row(2), row(3)
+    angle, weight = angle_ref[...], weight_ref[...]
     cos_det, sin_det = jnp.cos(2.0 * angle) * weight, jnp.sin(2.0 * angle) * weight
-    quad = 4.0 * small_ref[starts[1] : starts[1] + lines[1]]
+    quad = 4.0 * plate_ref[...]
     cos_plate, sin_plate = jnp.cos(quad), jnp.sin(quad)
     for part in range(samples // LANES):
         span = slice(part * LANES, (part + 1) * LANES)
@@ -83,8 +78,8 @@
         factor_ref[0, span] = jnp.broadcast_to(weight, (LANES, dets))
         factor_ref[1, span] = cos_p * cos_det - sin_p * sin_det
         factor_ref[2, span] = sin_p * cos_det + cos_p * sin_det
-    last = small_ref[starts[4] : starts[4] + 1]
-    owner, block = last[:, :tiles].astype(jnp.int32), last[:, tiles : 2 * tiles].astype(jnp.int32)
+    owner, block = owner_ref[...], block_ref[...]
+    tiles = owner.shape[1]
     shift = int(math.log2(col_blocks))
     map_row = owner * rows_own + lax.shift_right_logical(block, shift)
     map_col = block & (col_blocks - 1)
@@ -116,7 +111,7 @@
     reach,
     place_ref, partner_ref, outside_ref, band_ref, factor_ref, high_ref, right_ref, own_ref, index_ref,
     out_ref,
-    window, stokes, left,
+    window, stokes, left_even, left_odd,
 ):
     samples, dets = own_ref.shape
     groups = dets // LANES
@@ -145,24 +140,23 @@
     pieces = GROUP // groups
     mine = lax.div(iota((HIGH, LANES), 1), LOW) == iota((HIGH, LANES), 0)
     stack = GROUP * HIGH
-
-    def group_step(g, carry):
-        def piece_step(p, inner):
-            first = (g * pieces + p) * PIECE
+    tiles = (out_ref.shape[0] - index_ref.shape[0]) // 3
+
+    def build(g, left):
+        for p in range(pieces):
             for t in range(PIECE):
-                row = pl.ds(first + t, 1)
-                lanes = slice(t * LANES, (t + 1) * LANES)
+                k = (g * pieces + p) * PIECE + t
+                row, lanes = slice(k, k + 1), slice(t * LANES, (t + 1) * LANES)
                 hot = jnp.broadcast_to(high_ref[row, :], (HIGH, dets)) == high_ids
                 for s in range(3):
                     spread = jnp.where(hot, jnp.broadcast_to(stokes[s, row, :], (HIGH, dets)), 0.0)
                     both = jnp.concatenate(
-                        [spread[:, k * LANES : (k + 1) * LANES] for k in range(groups)], axis=0
+                        [spread[:, j * LANES : (j + 1) * LANES] for j in range(groups)], axis=0
                     )
-                    at = pl.multiple_of(s * stack + p * (groups * HIGH), groups * HIGH)
-                    left[pl.ds(at, groups * HIGH), lanes] = both.astype(BF16)
-            return inner
-
-        lax.fori_loop(0, pieces, piece_step, 0)
+                    at = s * stack + p * groups * HIGH
+                    left[at : at + groups * HIGH, lanes] = both.astype(BF16)
+
+    def collect(g, left):
         sums = lax.dot_general(left[...], right_ref[g], NT, preferred_element_type=F32)
         for s in range(3):
             rows = []
@@ -173,14 +167,16 @@
                     part = pltpu.roll(part, (start - i * LOW) % LANES, axis=1)
                 part = pltpu.roll(part, 0, axis=1, stride=LOW, stride_axis=0)
                 rows.append(jnp.sum(jnp.where(mine, part, 0.0), axis=0, keepdims=True))
-            out_ref[pl.ds(pl.multiple_of(g * GROUP, GROUP), GROUP), s * LANES : (s + 1) * LANES] = (
-                jnp.concatenate(rows, axis=0)
-            )
-        return carry
-
-    tiles = out_ref.shape[0] - index_ref.shape[0]
-    lax.fori_loop(0, tiles // GROUP, group_step, 0)
-    out_ref[tiles:] = index_ref[...]
+            at = s * tiles + g * GROUP
+            out_ref[at : at + GROUP] = jnp.concatenate(rows, axis=0)
+
+    lefts = (left_even, left_odd)
+    build(0, lefts[0])
+    for g in range(tiles // GROUP):
+        if (g + 1) * GROUP < tiles:
+            build(g + 1, lefts[(g + 1) % 2])
+        collect(g, lefts[g % 2])
+    out_ref[3 * tiles :] = index_ref[...]
 
 
 def table_kernel(place_ref, wiener_ref, ready_ref, held_ref, turns_ref, sem):
@@ -211,10 +207,13 @@
     def build(p, carry):
         rows = pl.ds(pl.multiple_of(p * LANES, LANES), LANES)
         low, high = stack_ref.at[2 * p], stack_ref.at[2 * p + 1]
-        tiles[pl.ds(pl.multiple_of(p * LANES, LANES), held)] = low[:held]
-        tiles[pl.ds(pl.multiple_of(p * LANES + held, held), held)] = high[:held]
-        r = jnp.where(left_side, low[held : held + 1, :LANES], high[held : held + 1, :LANES])
-        b = jnp.where(left_side, low[held + 1 : held + 2, :LANES], high[held + 1 : held + 2, :LANES])
+        for s in range(3):
+            channel, some = slice(s * LANES, (s + 1) * LANES), slice(s * held, (s + 1) * held)
+            tiles[pl.ds(pl.multiple_of(p * LANES, LANES), held), channel] = low[some]
+            tiles[pl.ds(pl.multiple_of(p * LANES + held, held), held), channel] = high[some]
+        at = 3 * held
+        r = jnp.where(left_side, low[at : at + 1], high[at : at + 1])
+        b = jnp.where(left_side, low[at + 1 : at + 2], high[at + 1 : at + 2])
         kx = first + iota((repeat, LANES), 0)
         c, s = turn((r.astype(jnp.int32) - kx * b.astype(jnp.int32) * LANES) & half_turns, 2 * ROWS)
         phases[0, :, rows] = c
@@ -373,19 +372,13 @@
     count_taps = kernel.shape[0]
     reach = (count_taps - 1) // 2
     width = count_taps - 1 + LANES
-    pieces = [
-        jnp.pad(kernel.astype(F32), (0, width - count_taps)), plate_angle, detector_angle, detector_weight,
-        tile_owner.reshape(tiles).astype(F32), tile_block.reshape(tiles).astype(F32),
-    ]
-    used = sum(piece.shape[0] for piece in pieces)
-    small = jnp.pad(jnp.concatenate(pieces), (0, -used % (8 * LANES))).reshape(-1, LANES)
     rows_own = ROWS // devices
     col_blocks = COLS // LANES
     vmem, hbm = pl.BlockSpec(memory_space=pltpu.VMEM), pl.BlockSpec(memory_space=pltpu.HBM)
     scalar = pl.BlockSpec(memory_space=pltpu.SMEM)
     place = lax.axis_index("tm").astype(jnp.int32).reshape(1)
     prepared = pl.pallas_call(
-        functools.partial(prepare_kernel, rows_own, col_blocks, tiles),
+        functools.partial(prepare_kernel, rows_own, col_blocks),
         out_specs=[vmem] * 6,
         out_shape=[
             pltpu.VMEM((LANES, width), BF16),
@@ -393,23 +386,28 @@
             pltpu.VMEM((samples, dets), jnp.int32),
             pltpu.VMEM((tiles // GROUP, GROUP * LOW, PIECE * LANES), BF16),
             pltpu.VMEM((samples, dets), BF16),
-            pltpu.VMEM((8, 3 * LANES), F32),
+            pltpu.VMEM((8, LANES), F32),
         ],
-        scratch_shapes=[pltpu.VMEM((samples, dets), jnp.int32)],
-        compiler_params=pltpu.CompilerParams(vmem_limit_bytes=32 * 2**20),
+        scratch_shapes=[pltpu.VMEM((samples, dets), jnp.int32), pltpu.VMEM((1, width), F32)],
+        compiler_params=pltpu.CompilerParams(vmem_limit_bytes=56 * 2**20),
         cost_estimate=pl.CostEstimate(flops=0, bytes_accessed=2**23, transcendentals=0),
         name="prepare",
-    )(pointing, timeline, small)
+    )(
+        pointing, timeline, kernel.reshape(1, count_taps), plate_angle.reshape(samples // LANES, LANES),
+        detector_angle.reshape(1, dets), detector_weight.reshape(1, dets),
+        tile_owner.reshape(1, tiles), tile_block.reshape(1, tiles),
+    )
     packed = pl.pallas_call(
         functools.partial(bin_kernel, reach),
         in_specs=[scalar] + [vmem] * 8,
-        out_shape=jax.ShapeDtypeStruct((tiles + 8, 3 * LANES), F32),
+        out_shape=jax.ShapeDtypeStruct((3 * tiles + 8, LANES), F32),
         scratch_shapes=[
             pltpu.VMEM((2 * reach + samples, dets), BF16),
             pltpu.VMEM((3, samples, dets), F32),
             pltpu.VMEM((3 * GROUP * HIGH, PIECE * LANES), BF16),
+            pltpu.VMEM((3 * GROUP * HIGH, PIECE * LANES), BF16),
         ],
-        compiler_params=pltpu.CompilerParams(vmem_limit_bytes=40 * 2**20),
+        compiler_params=pltpu.CompilerParams(vmem_limit_bytes=16 * 2**20),
         name="bin_tiles",
     )(place, partner, outside, *[pltpu.with_memory_space_constraint(v, pltpu.VMEM) for v in prepared])
     stokes, count, ky = wiener.shape
@@ -460,7 +458,7 @@
             pltpu.SemaphoreType.DMA((2, 2, 3)),
         ],
         out_shape=jax.ShapeDtypeStruct((2, stokes, count, ky), F32),
-        compiler_params=pltpu.CompilerParams(vmem_limit_bytes=40 * 2**20),
+        compiler_params=pltpu.CompilerParams(vmem_limit_bytes=16 * 2**20),
         name="spectra",
     )
     return sum(spectra(place, stack, held, turns, *more) for stack in stacks)

time: 45.4 us -> 41.2 us (0.907)
  local copies, waits for them, and re-layouts: 8.13 us -> 5.86 us
  other arithmetic: 1.4 us -> 0.03 us
  Pallas kernels: 23.8 us -> 22.6 us
  starting transfers between devices: 8.72 us -> 9.28 us
    unnamed x8 -> x2, local copies, waits for them, and re-layouts: 7.34 us -> 4.58 us
    pallas_call x1, Pallas kernels: 5.78 us -> 4.12 us  [body(): pl.pallas_call(functools.partial(bin_kernel, reach), in_specs=[scalar] +...]
    reshape x1, local copies, waits for them, and re-layouts: 0.01 us -> 1.28 us  [body(): kernel.reshape(1, count_taps)]
    pallas_call x1, Pallas kernels: 1.9 us -> 3.13 us  [body(): pl.pallas_call(functools.partial(prepare_kernel, rows_own, col_blocks), o...]
    ppermute x3, starting transfers between devices: 7.08 us -> 8.05 us  [gather(): lax.ppermute(value, axis, [(i, i ^ 2 * k) for i in range(size)])]
    concatenate x1 -> x0, local copies, waits for them, and re-layouts: 0.78 us -> none  [body(): jnp.concatenate(pieces)]
    pallas_call x1, Pallas kernels: 13.5 us -> 12.7 us  [body(): return sum((spectra(place, stack, held, turns, *more) for stack in stacks))]
    pad x1 -> x0, other arithmetic: 0.69 us -> none  [body(): jnp.pad(kernel.astype(F32), (0, width - count_taps))]
  transfers between devices with their start and end apart: 6 -> 6, of which waited for: 2 -> 2; matrix products, arithmetic and copies ran while one was open for 5% -> 3% of each run, Pallas kernels for 10% -> 14%
where the time goes in v4:
time: 41.2 us; the launch traced here: 41 us
  Pallas kernels  22.6 us (55%)
  starting transfers between devices  9.28 us (23%)
  local copies, waits for them, and re-layouts  5.86 us (14%)
  waiting for transfers between devices  3.17 us (8%)
    pallas_call x1, Pallas kernels, body(): return sum((spectra(place, stack, held, turns, *more) for stack in stacks))  12.7 us
    ppermute x3, starting transfers between devices, gather(): lax.ppermute(value, axis, [(i, i ^ 2 * k) for i in range(size)])  8.05 us
    unnamed x2, local copies, waits for them, and re-layouts  4.58 us
    pallas_call x1, Pallas kernels, body(): pl.pallas_call(functools.partial(bin_kernel, reach), in_specs=[scalar] +...  4.12 us
    pallas_call x1, Pallas kernels, body(): pl.pallas_call(functools.partial(prepare_kernel, rows_own, col_blocks), o...  3.13 us
    ppermute x3, waiting for transfers between devices, gather(): lax.ppermute(value, axis, [(i, i ^ 2 * k) for i in range(size)])  2.75 us
    pallas_call x1, Pallas kernels, body(): pl.pallas_call(table_kernel, in_specs=[scalar, hbm, pl.BlockSpec(memory_s...  1.31 us
    pallas_call x1, Pallas kernels, body(): pl.pallas_call(functools.partial(early_kernel, block), in_specs=[scalar,...  1.31 us
  transfers between devices with their start and end apart: 6, of which 2 were waited for; matrix products, arithmetic and copies ran while one was open for 3% of the time, Pallas kernels for 14%

profile of v4, /device:TPU:0, one launch (start us, length us, event | category | flops | bytes accessed | tf_op | source)
XLA Modules:
  0.0 41.0 jit_solution(8585413550725205478)
XLA Ops:
  0.0 0.5 %collective-permute-start = (bf16[512,256]{1,0:T(8,128)(2,1)}, bf16[512,256]{1,0:T(8,128)(2,1)S(1)}, u32[]{:S(2)}, u32[]{:S(2)}) collective-permute-start(bf16[512,256]{1,0:T(8,128)(2,1)} %time_ref.1), channel_id=1, source_target_pairs={{0,1},{1,0},{2,3},{3,2},{4,5},{5,4},{6,7},{7,6},{8,9},{9,8},{10,11... | collective-permute-start | bytes 786440 | tf_op jit(solution)/shard_map/ppermute | solution.py:348
  0.5 0.7 %collective-permute-start.1 = (bf16[512,256]{1,0:T(8,128)(2,1)}, bf16[512,256]{1,0:T(8,128)(2,1)S(1)}, u32[]{:S(2)}, u32[]{:S(2)}) collective-permute-start(bf16[512,256]{1,0:T(8,128)(2,1)} %time_ref.1), channel_id=1, source_target_pairs={{1,2},{3,4},{5,6},{2,1},{4,3},{6,5},{9,10},{11,12},{13,14},{10,9},... | collective-permute-start | bytes 786440 | tf_op jit(solution)/shard_map/ppermute | solution.py:347
  1.2 1.3 %reshape.22.kernel_ref = bf16[1,1025]{1,0:T(2,128)(2,1)} reshape(bf16[1025]{0:T(1024)(128)(2,1)} %param.14) | data formatting | bytes 4100 | tf_op jit(solution)/shard_map/reshape | solution.py:396
  2.5 3.1 %prepare.1 = (bf16[128,1152]{1,0:T(8,128)(2,1)S(1)}, f32[3,512,256]{2,1,0:T(8,128)S(1)}, s32[512,256]{1,0:T(8,128)S(1)}, bf16[4,256,2048]{2,1,0:T(8,128)(2,1)S(1...) custom-call(s32[512,256]{1,0:T(8,128)} %pixel_ref.1, bf16[512,256]{1,0:T(8,128)(2,1)} %time_ref.1, ...), custom_call_target="tpu_custom_call" | custom-call | bytes 8388608 | tf_op jit(solution)/shard_map/prepare/pallas_call | solution.py:380
  5.6 0.0 collective-permute-done.partner_ref
  5.6 0.0 collective-permute-done.1.outside_ref
  5.6 4.1 %bin_tiles.1.ready_ref = f32[200,128]{1,0:T(8,128)S(1)} custom-call(s32[1]{0:T(128)} %bitcast.place_ref, bf16[512,256]{1,0:T(8,128)(2,1)S(1)} %collective-permute-done.partner_ref, bf16[512,256]{1,0:T(8,128)(2,1)S(1)} %collective-permute-done.1.outside_ref, bf16[128,1152]{1,0:T(8,128)(2,1)S(1)} %get-tuple-element.16.band_ref, ...), custom_call_target="tpu_custom_call" | custom-call | tf_op jit(solution)/shard_map/bin_tiles/pallas_call | solution.py:400
  9.7 7.4 %collective-permute-start.4 = (f32[200,128]{1,0:T(8,128)S(1)}, f32[200,128]{1,0:T(8,128)S(1)}, u32[]{:S(2)}, u32[]{:S(2)}) collective-permute-start(f32[200,128]{1,0:T(8,128)S(1)} %bin_tiles.1.ready_ref), channel_id=1, source_target_pairs={{0,6},{1,7},{2,4},{3,5},{4,2},{5,3},{6,0},{7,1},{8,14},{9,15},{10,... | collective-permute-start | bytes 307208 | tf_op jit(solution)/shard_map/ppermute | solution.py:358
  17.1 0.0 collective-permute-start.3
  17.1 0.6 %collective-permute-start.2 = (f32[200,128]{1,0:T(8,128)S(1)}, f32[200,128]{1,0:T(8,128)S(1)}, u32[]{:S(2)}, u32[]{:S(2)}) collective-permute-start(f32[200,128]{1,0:T(8,128)S(1)} %bin_tiles.1.ready_ref), channel_id=1, source_target_pairs={{0,2},{1,3},{2,0},{3,1},{4,6},{5,7},{6,4},{7,5},{8,10},{9,11},{10,... | collective-permute-start | bytes 307208 | tf_op jit(solution)/shard_map/ppermute | solution.py:358
  17.8 0.0 copy-start
  17.8 4.6 %copy-done = f32[3,512,2048]{2,1,0:T(8,128)S(1)} copy-done((f32[3,512,2048]{2,1,0:T(8,128)S(1)}, f32[3,512,2048]{2,1,0:T(8,128)}, u32[]{:S(2)}) %copy-start) | copy-done | bytes 12582936
  22.4 1.3 %tables.1 = (f32[3,512,2048]{2,1,0:T(8,128)S(1)}, bf16[2,512,256]{2,1,0:T(8,128)(2,1)S(1)}) custom-call(s32[1]{0:T(128)} %bitcast.place_ref, f32[3,512,2048]{2,1,0:T(8,128)S(1)} %copy-done, f32[200,128]{1,0:T(8,128)S(1)} %bin_tiles.1.ready_ref), custom_call_target="tpu_custom_call" | custom-call | bytes 25165824 | tf_op jit(solution)/shard_map/tables/pallas_call | solution.py:414
  23.7 0.0 collective-permute-done.4
  23.7 2.7 %collective-permute-done.3 = f32[200,128]{1,0:T(8,128)S(1)} collective-permute-done((f32[200,128]{1,0:T(8,128)S(1)}, f32[200,128]{1,0:T(8,128)S(1)}, u32[]{:S(2)}, u32[]{:S(2)}) %collective-permute-start.3) | collective-permute-done | bytes 102432 | tf_op jit(solution)/shard_map/ppermute | solution.py:358
  26.4 0.0 collective-permute-done.2
  26.5 0.1 collective-permute-start.5
  26.6 1.3 %early_factors.1 = (bf16[3,1024,256]{2,1,0:T(8,128)(2,1)S(1)}, bf16[256,2048]{1,0:T(8,128)(2,1)S(1)}) custom-call(s32[1]{0:T(128)} %bitcast.place_ref, f32[4,200,128]{2,1,0:T(8,128)S(1)} %pad_maximum_fusion.stack_ref, bf16[2,512,256]{2,1,0:T(8,128)(2,1)S(1)} %get-tuple-element.22.turns_ref), custom_call_target="tpu_custom_call" | custom-call | flops 603979776 | bytes 4194304 | tf_op jit(solution)/shard_map/early_factors/pallas_call | solution.py:434
  27.9 0.4 %collective-permute-done.5.stack_ref = f32[4,200,128]{2,1,0:T(8,128)S(1)} collective-permute-done((f32[4,200,128]{2,1,0:T(8,128)S(1)}, f32[4,200,128]{2,1,0:T(8,128)S(1)}, u32[]{:S(2)}, u32[]{:S(2)}) %collective-permute-start.5) | collective-permute-done | bytes 409632 | tf_op jit(solution)/shard_map/ppermute | solution.py:362
  28.3 12.7 %spectra.1 = f32[2,3,512,2048]{3,2,1,0:T(8,128)} custom-call(s32[1]{0:T(128)} %bitcast.place_ref, f32[4,200,128]{2,1,0:T(8,128)S(1)} %collective-permute-done.5.stack_ref, f32[3,512,2048]{2,1,0:T(8,128)S(1)} %get-tuple-element.24.wiener_ref, bf16[2,512,256]{2,1,0:T(8,128)(2,1)S(1)} %get-tuple-element.22.turns_ref, ...), custom_call_target="tpu_custom_call" | custom-call | tf_op jit(solution)/shard_map/spectra/pallas_call | solution.py:464
  (1 shorter events, 0.0 us)
Async XLA Ops:
  0.0 5.6 %collective-permute-start = (bf16[512,256]{1,0:T(8,128)(2,1)}, bf16[512,256]{1,0:T(8,128)(2,1)S(1)}, u32[]{:S(2)}, u32[]{:S(2)}) collective-permute-start(bf16[512,256]{1,0:T(8,128)(2,1)} %time_ref.1), channel_id=1, source_target_pairs={{0,1},{1,0},{2,3},{3,2},{4,5},{5,4},{6,7},{7,6},{8,9},{9,8},{10,11... | collective-permute-start | bytes 786440 | tf_op jit(solution)/shard_map/ppermute | solution.py:348
  0.5 5.1 %collective-permute-start.1 = (bf16[512,256]{1,0:T(8,128)(2,1)}, bf16[512,256]{1,0:T(8,128)(2,1)S(1)}, u32[]{:S(2)}, u32[]{:S(2)}) collective-permute-start(bf16[512,256]{1,0:T(8,128)(2,1)} %time_ref.1), channel_id=1, source_target_pairs={{1,2},{3,4},{5,6},{2,1},{4,3},{6,5},{9,10},{11,12},{13,14},{10,9},... | collective-permute-start | bytes 786440 | tf_op jit(solution)/shard_map/ppermute | solution.py:347
  9.7 14.0 %collective-permute-start.4 = (f32[200,128]{1,0:T(8,128)S(1)}, f32[200,128]{1,0:T(8,128)S(1)}, u32[]{:S(2)}, u32[]{:S(2)}) collective-permute-start(f32[200,128]{1,0:T(8,128)S(1)} %bin_tiles.1.ready_ref), channel_id=1, source_target_pairs={{0,6},{1,7},{2,4},{3,5},{4,2},{5,3},{6,0},{7,1},{8,14},{9,15},{10,... | collective-permute-start | bytes 307208 | tf_op jit(solution)/shard_map/ppermute | solution.py:358
  17.1 9.3 %collective-permute-start.3 = (f32[200,128]{1,0:T(8,128)S(1)}, f32[200,128]{1,0:T(8,128)S(1)}, u32[]{:S(2)}, u32[]{:S(2)}) collective-permute-start(f32[200,128]{1,0:T(8,128)S(1)} %bin_tiles.1.ready_ref), channel_id=1, source_target_pairs={{0,4},{1,5},{2,6},{3,7},{4,0},{5,1},{6,2},{7,3},{8,12},{9,13},{10,... | collective-permute-start | bytes 307208 | tf_op jit(solution)/shard_map/ppermute | solution.py:358
  17.1 9.3 %collective-permute-start.2 = (f32[200,128]{1,0:T(8,128)S(1)}, f32[200,128]{1,0:T(8,128)S(1)}, u32[]{:S(2)}, u32[]{:S(2)}) collective-permute-start(f32[200,128]{1,0:T(8,128)S(1)} %bin_tiles.1.ready_ref), channel_id=1, source_target_pairs={{0,2},{1,3},{2,0},{3,1},{4,6},{5,7},{6,4},{7,5},{8,10},{9,11},{10,... | collective-permute-start | bytes 307208 | tf_op jit(solution)/shard_map/ppermute | solution.py:358
  17.8 4.6 %copy-start = (f32[3,512,2048]{2,1,0:T(8,128)S(1)}, f32[3,512,2048]{2,1,0:T(8,128)}, u32[]{:S(2)}) copy-start(f32[3,512,2048]{2,1,0:T(8,128)} %wiener_ref.1) | copy-start | bytes 37748740
  26.5 1.8 %collective-permute-start.5 = (f32[4,200,128]{2,1,0:T(8,128)S(1)}, f32[4,200,128]{2,1,0:T(8,128)S(1)}, u32[]{:S(2)}, u32[]{:S(2)}) collective-permute-start(f32[4,200,128]{2,1,0:T(8,128)S(1)} %pad_maximum_fusion.stack_ref), channel_id=1, source_target_pairs={{0,1},{1,0},{2,3},{3,2},{4,5},{5,4},{6,7},{7,6},{8,9},{9,8},{10,11... | collective-permute-start | bytes 1228808 | tf_op jit(solution)/shard_map/ppermute | solution.py:362

commit v5 on v4

--- a/solution.py
+++ b/solution.py
@@ -263,7 +263,7 @@
 
 def spectrum_kernel(early, place_ref, stack_ref, wiener_ref, turns_ref, *refs):
     ready_factor, ready_table = refs[:2] if early else (None, None)
-    out_ref, tiles, factor, table, phases, buffer, sems = refs[2 * early :]
+    out_ref, tiles, factor, second, table, phases, buffer, sems = refs[2 * early :]
     stokes, count, ky = wiener_ref.shape
     block = factor.shape[0] // 2
     own = tiles.shape[0]
@@ -288,13 +288,15 @@
                     buffer.at[slot, side, :, lanes], out_ref.at[side, s, at, lanes], sems.at[slot, side, j]
                 )
 
-    def step(i, carry):
-        slot = lax.rem(i, 2)
+    def place_of(i):
         s, k = lax.div(i, count // block), lax.rem(i, count // block)
-        at = pl.ds(pl.multiple_of(k * block, block), block)
+        return s, k, pl.ds(pl.multiple_of(k * block, block), block)
+
+    def make(i, factor):
+        s, k, at = place_of(i)
         channel = pl.ds(pl.multiple_of(s * LANES, LANES), LANES)
 
-        def make(q, inner):
+        def some(q, inner):
             rows = pl.ds(pl.multiple_of(q * width, width), width)
             into = pl.ds(pl.multiple_of(ready + q * width, LANES), width)
             real, imag = factors(tiles, phases, turns_ref, rows, channel, at, block)
@@ -302,17 +304,25 @@
             factor[block:, into] = imag
             return inner
 
-        lax.fori_loop(0, own // width, make, 0)
+        if own == width:
+            some(0, 0)
+        else:
+            lax.fori_loop(0, own // width, some, 0)
         if early:
             under = pl.ds(pl.multiple_of(count + k * block, block), block)
             factor[:block, :ready] = ready_factor[s, at]
             factor[block:, :ready] = ready_factor[s, under]
 
+    def step(i, slot, factor, later):
+        s, k, at = place_of(i)
+
         @pl.when(i >= 2)
         def _():
             for copy in copies(i, slot, (0, 1, 2)):
                 copy.wait()
 
+        if later is not None:
+            make(lax.rem(i + 1, steps), later)
         for n in range(half // LANES):
             lanes = slice(n * LANES, (n + 1) * LANES)
             back = slice(ky - (n + 1) * LANES, ky - n * LANES)
@@ -332,10 +342,18 @@
                     copy.start()
         for copy in copies(i, slot, (2,)):
             copy.start()
+
+    steps = stokes * (count // block)
+    make(jnp.int32(0), factor)
+
+    def pair(j, carry):
+        step(2 * j, 0, factor, second)
+        step(2 * j + 1, 1, second, factor)
         return carry
 
-    steps = stokes * (count // block)
-    lax.fori_loop(0, steps, step, 0)
+    lax.fori_loop(0, steps // 2, pair, 0)
+    if steps % 2:
+        step(jnp.int32(steps - 1), 0, factor, None)
     for i in (steps - 2, steps - 1):
         for copy in copies(i, i % 2, (0, 1, 2)):
             copy.wait()
@@ -452,6 +470,7 @@
         scratch_shapes=[
             lists[0],
             pltpu.VMEM((2 * block, columns), BF16),
+            pltpu.VMEM((2 * block, columns), BF16),
             pltpu.VMEM((columns, ky), BF16),
             lists[1],
             pltpu.VMEM((2, 2, block, ky), F32),

time: 41.2 us -> 40.4 us (0.981)
  Pallas kernels: 22.6 us -> 21.8 us
    pallas_call x1, Pallas kernels: 12.7 us -> 11.9 us  [body(): return sum((spectra(place, stack, held, turns, *more) for stack in stacks))]
where the time goes in v5:
time: 40.4 us; the launch traced here: 40.2 us
  Pallas kernels  21.8 us (54%)
  starting transfers between devices  9.28 us (23%)
  local copies, waits for them, and re-layouts  5.86 us (15%)
  waiting for transfers between devices  3.17 us (8%)
    pallas_call x1, Pallas kernels, body(): return sum((spectra(place, stack, held, turns, *more) for stack in stacks))  11.9 us
    ppermute x3, starting transfers between devices, gather(): lax.ppermute(value, axis, [(i, i ^ 2 * k) for i in range(size)])  8.05 us
    unnamed x2, local copies, waits for them, and re-layouts  4.58 us
    pallas_call x1, Pallas kernels, body(): pl.pallas_call(functools.partial(bin_kernel, reach), in_specs=[scalar] +...  4.12 us
    pallas_call x1, Pallas kernels, body(): pl.pallas_call(functools.partial(prepare_kernel, rows_own, col_blocks), o...  3.13 us
    ppermute x3, waiting for transfers between devices, gather(): lax.ppermute(value, axis, [(i, i ^ 2 * k) for i in range(size)])  2.75 us
    pallas_call x1, Pallas kernels, body(): pl.pallas_call(table_kernel, in_specs=[scalar, hbm, pl.BlockSpec(memory_s...  1.31 us
    pallas_call x1, Pallas kernels, body(): pl.pallas_call(functools.partial(early_kernel, block), in_specs=[scalar,...  1.31 us
  transfers between devices with their start and end apart: 6, of which 2 were waited for; matrix products, arithmetic and copies ran while one was open for 3% of the time, Pallas kernels for 14%

profile of v5, /device:TPU:0, one launch (start us, length us, event | category | flops | bytes accessed | tf_op | source)
XLA Modules:
  0.0 40.2 jit_solution(5563354385951442701)
XLA Ops:
  0.0 0.5 %collective-permute-start = (bf16[512,256]{1,0:T(8,128)(2,1)}, bf16[512,256]{1,0:T(8,128)(2,1)S(1)}, u32[]{:S(2)}, u32[]{:S(2)}) collective-permute-start(bf16[512,256]{1,0:T(8,128)(2,1)} %time_ref.1), channel_id=1, source_target_pairs={{0,1},{1,0},{2,3},{3,2},{4,5},{5,4},{6,7},{7,6},{8,9},{9,8},{10,11... | collective-permute-start | bytes 786440 | tf_op jit(solution)/shard_map/ppermute | solution.py:366
  0.5 0.7 %collective-permute-start.1 = (bf16[512,256]{1,0:T(8,128)(2,1)}, bf16[512,256]{1,0:T(8,128)(2,1)S(1)}, u32[]{:S(2)}, u32[]{:S(2)}) collective-permute-start(bf16[512,256]{1,0:T(8,128)(2,1)} %time_ref.1), channel_id=1, source_target_pairs={{1,2},{3,4},{5,6},{2,1},{4,3},{6,5},{9,10},{11,12},{13,14},{10,9},... | collective-permute-start | bytes 786440 | tf_op jit(solution)/shard_map/ppermute | solution.py:365
  1.2 1.3 %reshape.22.kernel_ref = bf16[1,1025]{1,0:T(2,128)(2,1)} reshape(bf16[1025]{0:T(1024)(128)(2,1)} %param.14) | data formatting | bytes 4100 | tf_op jit(solution)/shard_map/reshape | solution.py:414
  2.5 3.1 %prepare.1 = (bf16[128,1152]{1,0:T(8,128)(2,1)S(1)}, f32[3,512,256]{2,1,0:T(8,128)S(1)}, s32[512,256]{1,0:T(8,128)S(1)}, bf16[4,256,2048]{2,1,0:T(8,128)(2,1)S(1...) custom-call(s32[512,256]{1,0:T(8,128)} %pixel_ref.1, bf16[512,256]{1,0:T(8,128)(2,1)} %time_ref.1, ...), custom_call_target="tpu_custom_call" | custom-call | bytes 8388608 | tf_op jit(solution)/shard_map/prepare/pallas_call | solution.py:398
  5.6 0.0 collective-permute-done.partner_ref
  5.6 0.0 collective-permute-done.1.outside_ref
  5.6 4.1 %bin_tiles.1.ready_ref = f32[200,128]{1,0:T(8,128)S(1)} custom-call(s32[1]{0:T(128)} %bitcast.place_ref, bf16[512,256]{1,0:T(8,128)(2,1)S(1)} %collective-permute-done.partner_ref, bf16[512,256]{1,0:T(8,128)(2,1)S(1)} %collective-permute-done.1.outside_ref, bf16[128,1152]{1,0:T(8,128)(2,1)S(1)} %get-tuple-element.16.band_ref, ...), custom_call_target="tpu_custom_call" | custom-call | tf_op jit(solution)/shard_map/bin_tiles/pallas_call | solution.py:418
  9.7 7.4 %collective-permute-start.4 = (f32[200,128]{1,0:T(8,128)S(1)}, f32[200,128]{1,0:T(8,128)S(1)}, u32[]{:S(2)}, u32[]{:S(2)}) collective-permute-start(f32[200,128]{1,0:T(8,128)S(1)} %bin_tiles.1.ready_ref), channel_id=1, source_target_pairs={{0,6},{1,7},{2,4},{3,5},{4,2},{5,3},{6,0},{7,1},{8,14},{9,15},{10,... | collective-permute-start | bytes 307208 | tf_op jit(solution)/shard_map/ppermute | solution.py:376
  17.1 0.0 collective-permute-start.3
  17.1 0.6 %collective-permute-start.2 = (f32[200,128]{1,0:T(8,128)S(1)}, f32[200,128]{1,0:T(8,128)S(1)}, u32[]{:S(2)}, u32[]{:S(2)}) collective-permute-start(f32[200,128]{1,0:T(8,128)S(1)} %bin_tiles.1.ready_ref), channel_id=1, source_target_pairs={{0,2},{1,3},{2,0},{3,1},{4,6},{5,7},{6,4},{7,5},{8,10},{9,11},{10,... | collective-permute-start | bytes 307208 | tf_op jit(solution)/shard_map/ppermute | solution.py:376
  17.8 0.0 copy-start
  17.8 4.6 %copy-done = f32[3,512,2048]{2,1,0:T(8,128)S(1)} copy-done((f32[3,512,2048]{2,1,0:T(8,128)S(1)}, f32[3,512,2048]{2,1,0:T(8,128)}, u32[]{:S(2)}) %copy-start) | copy-done | bytes 12582936
  22.4 1.3 %tables.1 = (f32[3,512,2048]{2,1,0:T(8,128)S(1)}, bf16[2,512,256]{2,1,0:T(8,128)(2,1)S(1)}) custom-call(s32[1]{0:T(128)} %bitcast.place_ref, f32[3,512,2048]{2,1,0:T(8,128)S(1)} %copy-done, f32[200,128]{1,0:T(8,128)S(1)} %bin_tiles.1.ready_ref), custom_call_target="tpu_custom_call" | custom-call | bytes 25165824 | tf_op jit(solution)/shard_map/tables/pallas_call | solution.py:432
  23.7 0.0 collective-permute-done.4
  23.7 2.7 %collective-permute-done.3 = f32[200,128]{1,0:T(8,128)S(1)} collective-permute-done((f32[200,128]{1,0:T(8,128)S(1)}, f32[200,128]{1,0:T(8,128)S(1)}, u32[]{:S(2)}, u32[]{:S(2)}) %collective-permute-start.3) | collective-permute-done | bytes 102432 | tf_op jit(solution)/shard_map/ppermute | solution.py:376
  26.4 0.0 collective-permute-done.2
  26.5 0.1 collective-permute-start.5
  26.6 1.3 %early_factors.1 = (bf16[3,1024,256]{2,1,0:T(8,128)(2,1)S(1)}, bf16[256,2048]{1,0:T(8,128)(2,1)S(1)}) custom-call(s32[1]{0:T(128)} %bitcast.place_ref, f32[4,200,128]{2,1,0:T(8,128)S(1)} %pad_maximum_fusion.stack_ref, bf16[2,512,256]{2,1,0:T(8,128)(2,1)S(1)} %get-tuple-element.22.turns_ref), custom_call_target="tpu_custom_call" | custom-call | flops 603979776 | bytes 4194304 | tf_op jit(solution)/shard_map/early_factors/pallas_call | solution.py:452
  27.9 0.4 %collective-permute-done.5.stack_ref = f32[4,200,128]{2,1,0:T(8,128)S(1)} collective-permute-done((f32[4,200,128]{2,1,0:T(8,128)S(1)}, f32[4,200,128]{2,1,0:T(8,128)S(1)}, u32[]{:S(2)}, u32[]{:S(2)}) %collective-permute-start.5) | collective-permute-done | bytes 409632 | tf_op jit(solution)/shard_map/ppermute | solution.py:380
  28.3 11.9 %spectra.1 = f32[2,3,512,2048]{3,2,1,0:T(8,128)} custom-call(s32[1]{0:T(128)} %bitcast.place_ref, f32[4,200,128]{2,1,0:T(8,128)S(1)} %collective-permute-done.5.stack_ref, f32[3,512,2048]{2,1,0:T(8,128)S(1)} %get-tuple-element.24.wiener_ref, bf16[2,512,256]{2,1,0:T(8,128)(2,1)S(1)} %get-tuple-element.22.turns_ref, ...), custom_call_target="tpu_custom_call" | custom-call | tf_op jit(solution)/shard_map/spectra/pallas_call | solution.py:483
  (1 shorter events, 0.0 us)
Async XLA Ops:
  0.0 5.6 %collective-permute-start = (bf16[512,256]{1,0:T(8,128)(2,1)}, bf16[512,256]{1,0:T(8,128)(2,1)S(1)}, u32[]{:S(2)}, u32[]{:S(2)}) collective-permute-start(bf16[512,256]{1,0:T(8,128)(2,1)} %time_ref.1), channel_id=1, source_target_pairs={{0,1},{1,0},{2,3},{3,2},{4,5},{5,4},{6,7},{7,6},{8,9},{9,8},{10,11... | collective-permute-start | bytes 786440 | tf_op jit(solution)/shard_map/ppermute | solution.py:366
  0.5 5.1 %collective-permute-start.1 = (bf16[512,256]{1,0:T(8,128)(2,1)}, bf16[512,256]{1,0:T(8,128)(2,1)S(1)}, u32[]{:S(2)}, u32[]{:S(2)}) collective-permute-start(bf16[512,256]{1,0:T(8,128)(2,1)} %time_ref.1), channel_id=1, source_target_pairs={{1,2},{3,4},{5,6},{2,1},{4,3},{6,5},{9,10},{11,12},{13,14},{10,9},... | collective-permute-start | bytes 786440 | tf_op jit(solution)/shard_map/ppermute | solution.py:365
  9.7 14.0 %collective-permute-start.4 = (f32[200,128]{1,0:T(8,128)S(1)}, f32[200,128]{1,0:T(8,128)S(1)}, u32[]{:S(2)}, u32[]{:S(2)}) collective-permute-start(f32[200,128]{1,0:T(8,128)S(1)} %bin_tiles.1.ready_ref), channel_id=1, source_target_pairs={{0,6},{1,7},{2,4},{3,5},{4,2},{5,3},{6,0},{7,1},{8,14},{9,15},{10,... | collective-permute-start | bytes 307208 | tf_op jit(solution)/shard_map/ppermute | solution.py:376
  17.1 9.3 %collective-permute-start.3 = (f32[200,128]{1,0:T(8,128)S(1)}, f32[200,128]{1,0:T(8,128)S(1)}, u32[]{:S(2)}, u32[]{:S(2)}) collective-permute-start(f32[200,128]{1,0:T(8,128)S(1)} %bin_tiles.1.ready_ref), channel_id=1, source_target_pairs={{0,4},{1,5},{2,6},{3,7},{4,0},{5,1},{6,2},{7,3},{8,12},{9,13},{10,... | collective-permute-start | bytes 307208 | tf_op jit(solution)/shard_map/ppermute | solution.py:376
  17.1 9.3 %collective-permute-start.2 = (f32[200,128]{1,0:T(8,128)S(1)}, f32[200,128]{1,0:T(8,128)S(1)}, u32[]{:S(2)}, u32[]{:S(2)}) collective-permute-start(f32[200,128]{1,0:T(8,128)S(1)} %bin_tiles.1.ready_ref), channel_id=1, source_target_pairs={{0,2},{1,3},{2,0},{3,1},{4,6},{5,7},{6,4},{7,5},{8,10},{9,11},{10,... | collective-permute-start | bytes 307208 | tf_op jit(solution)/shard_map/ppermute | solution.py:376
  17.8 4.6 %copy-start = (f32[3,512,2048]{2,1,0:T(8,128)S(1)}, f32[3,512,2048]{2,1,0:T(8,128)}, u32[]{:S(2)}) copy-start(f32[3,512,2048]{2,1,0:T(8,128)} %wiener_ref.1) | copy-start | bytes 37748740
  26.5 1.8 %collective-permute-start.5 = (f32[4,200,128]{2,1,0:T(8,128)S(1)}, f32[4,200,128]{2,1,0:T(8,128)S(1)}, u32[]{:S(2)}, u32[]{:S(2)}) collective-permute-start(f32[4,200,128]{2,1,0:T(8,128)S(1)} %pad_maximum_fusion.stack_ref), channel_id=1, source_target_pairs={{0,1},{1,0},{2,3},{3,2},{4,5},{5,4},{6,7},{7,6},{8,9},{9,8},{10,11... | collective-permute-start | bytes 1228808 | tf_op jit(solution)/shard_map/ppermute | solution.py:380
